TPU v7x, 32 devices: a whole 2x2x4 slice. The times are simulated.
32 devices in a mesh: scan: 8 (over y, x, core), tile: 4 (over z).
Axes of the slice: x: 2, y: 2, z: 4, core: 2. Of those that a mesh axis runs over, the one named last changes fastest.
Arguments:
- object_field: float32 [2, 2048, 1024], P(None, 'scan', 'tile'), may hold values from -4.2 to 4.2
- probe_modes: float32 [8, 2, 256, 256], P('tile'), may hold values from -2.1 to 2.1
- amplitudes: bfloat16 [64, 256, 256], P('scan'), may hold values from 0.25 to 3
- positions: int32 [64, 2], P('scan'), may hold values from 0 to 1792, as said below
- counts: int32 [8], P('scan'), may hold values from 1 to 8, as said below
Outputs:
- new_object: float32 [2, 2048, 1024], P(None, 'scan', 'tile')
- probe_step: float32 [8, 2, 256, 256], P('tile')
Inputs may be any that keep to these rules, and one draw needn't show every extreme that they name: `positions`: slot j's row offset lies in rows (j // 8) * 256 to (j // 8) * 256 + 255; every window lies inside the object: row offsets at most 1792, column offsets at most 768. `counts`: some scan index holds 8 live slots and some holds one.
All inputs are finite; a program needn't handle non-finite values.
Results may differ from a plain program's by a relative error of at most 0.003.
Values may be sent and summed in bfloat16 or wider, within the bound.
No kernel may reach another device: no remote copies, remote signals or barrier semaphores. Data moves between devices by JAX's collectives and lax.ppermute only.
A program may use at most 128 MiB of HBM per device.

v0:
```python
import math

import jax
import jax.numpy as jnp
from jax import lax
from jax.sharding import PartitionSpec as P

damping = 1.0
amp_floor = 0.5


def passed_along(value, axis, steps):
    count = lax.axis_size(axis)
    leading, last = (max(0, -steps), min(count, count - steps))
    return lax.ppermute(value, axis, [(source, source + steps) for source in range(leading, last)])


def dft_tables(win_width):
    index_row = jnp.arange(win_width, dtype=jnp.int32)
    products = index_row[:, None] * index_row[None, :] % win_width
    phase_angle = products.astype(jnp.float32) * (2.0 * math.pi / win_width)
    norm_scale = 1.0 / math.sqrt(win_width)
    real_part = (jnp.cos(phase_angle) * norm_scale).astype(jnp.bfloat16)
    imag_part = (-jnp.sin(phase_angle) * norm_scale).astype(jnp.bfloat16)
    return (real_part, imag_part)


def transform(rowform, right_table, left_table, win_width):
    half_done = jnp.einsum(
        "mak,kl->mal", rowform, right_table, preferred_element_type=jnp.float32
    ).astype(jnp.bfloat16)
    full_block = jnp.einsum(
        "ca,mak->mck", left_table, half_done, preferred_element_type=jnp.float32
    )
    real_out = full_block[..., :win_width, :win_width] - full_block[..., win_width:, win_width:]
    imag_out = full_block[..., :win_width, win_width:] + full_block[..., win_width:, :win_width]
    return (real_out, imag_out)


def shards(object_field, probe_modes, amplitudes, positions, counts):
    slot_count = amplitudes.shape[0]
    win_width = amplitudes.shape[1]
    band_rows = object_field.shape[1]
    first_row = lax.axis_index("scan") * band_rows
    object_low = object_field.astype(jnp.bfloat16)
    lower_rows = passed_along(object_low, "scan", -1)
    extended = jnp.concatenate([object_low, lower_rows], axis=1)
    band_all = lax.all_gather(extended, "tile", axis=2, tiled=True)
    row_offsets = positions[:, 0] - first_row
    col_offsets = positions[:, 1]
    zero_index = jnp.zeros((), jnp.int32)

    def cut_window(row_at, col_at):
        return lax.dynamic_slice(band_all, (zero_index, row_at, col_at), (2, win_width, win_width))

    windows = jax.vmap(cut_window)(row_offsets, col_offsets)
    slot_ids = jnp.arange(slot_count, dtype=jnp.int32)
    live_mask = (slot_ids < counts[0]).astype(jnp.float32)
    real_part, imag_part = dft_tables(win_width)
    right_fwd = jnp.block([[real_part, imag_part], [-imag_part, real_part]])
    left_fwd = jnp.concatenate([real_part, imag_part], axis=0)
    right_inv = jnp.block([[real_part, -imag_part], [imag_part, real_part]])
    left_inv = jnp.concatenate([real_part, -imag_part], axis=0)
    probe_re = probe_modes[:, 0]
    probe_im = probe_modes[:, 1]
    probe_power = jnp.sum(probe_re * probe_re + probe_im * probe_im, axis=0)

    def forward_one(window):
        window_re = window[0].astype(jnp.float32)
        window_im = window[1].astype(jnp.float32)
        exit_wave = jnp.concatenate(
            [
                probe_re * window_re - probe_im * window_im,
                probe_re * window_im + probe_im * window_re,
            ],
            axis=-1,
        ).astype(jnp.bfloat16)
        far_re, far_im = transform(exit_wave, right_fwd, left_fwd, win_width)
        return (far_re, far_im, jnp.sum(far_re * far_re + far_im * far_im, axis=0))

    far_re, far_im, local_power = lax.map(forward_one, windows)
    intensity = lax.psum(local_power, "tile")
    factor = live_mask[:, None, None] * (
        amplitudes.astype(jnp.float32) / jnp.maximum(jnp.sqrt(intensity), amp_floor) - 1.0
    )
    channels = 3

    def accumulate(running, inputs):
        buffer, grad_sum, weight_sum = running
        slot_re, slot_im, slot_factor, window, live, row_at, col_at = inputs
        change = jnp.concatenate([slot_factor * slot_re, slot_factor * slot_im], axis=-1).astype(
            jnp.bfloat16
        )
        near_re, near_im = transform(change, right_inv, left_inv, win_width)
        window_re = window[0].astype(jnp.float32)
        window_im = window[1].astype(jnp.float32)
        numer_parts = [
            jnp.sum(probe_re * near_re + probe_im * near_im, axis=0),
            jnp.sum(probe_re * near_im - probe_im * near_re, axis=0),
        ]
        numer_parts.append(live * probe_power)
        numer = jnp.stack(numer_parts)
        grads = jnp.stack(
            [window_re * near_re + window_im * near_im, window_re * near_im - window_im * near_re],
            axis=1,
        )
        weight = window_re * window_re + window_im * window_im
        region = lax.dynamic_slice(
            buffer, (zero_index, row_at, col_at), (channels, win_width, win_width)
        )
        buffer = lax.dynamic_update_slice(buffer, region + numer, (zero_index, row_at, col_at))
        return ((buffer, grad_sum + grads, weight_sum + live * weight), None)

    init = (
        jnp.zeros((channels, band_rows + win_width, band_all.shape[2]), jnp.float32),
        jnp.zeros(probe_modes.shape, jnp.float32),
        jnp.zeros((win_width, win_width), jnp.float32),
    )
    (buffer, grad_sum, weight_sum), _ = lax.scan(
        accumulate, init, (far_re, far_im, factor, windows, live_mask, row_offsets, col_offsets)
    )
    rim_rows = passed_along(buffer[:, band_rows:, :].astype(jnp.bfloat16), "scan", 1).astype(
        jnp.float32
    )
    own_rows = buffer[:, :band_rows, :].at[:, :win_width, :].add(rim_rows)
    totals = lax.psum_scatter(own_rows, "tile", scatter_dimension=2, tiled=True)
    illumination = totals[2]
    new_object = object_field + totals[0:2] / (illumination + damping)[None]
    grad_total, weight_total = lax.psum((grad_sum, weight_sum), "scan")
    probe_step = grad_total / (weight_total + damping)[None, None]
    return (new_object, probe_step)


def solution(mesh):
    placed = (
        P(None, "scan", "tile"),
        P("tile", None, None, None),
        P("scan", None, None),
        P("scan", None),
        P("scan"),
    )
    return jax.shard_map(
        shards,
        mesh=mesh,
        in_specs=placed,
        out_specs=(P(None, "scan", "tile"), P("tile", None, None, None)),
        check_vma=False,
    )
```

profile of v0, /device:TPU:0, one launch (start us, length us, event | category | flops | bytes accessed | tf_op | source)
XLA Modules:
  0.0 642.8 jit_solution(17734044107008832897)
XLA Ops:
  18.0 47.6 %all-gather.2.cloned.1.call-done = bf16[2,512,1024]{2,1,0:T(8,128)(2,1)} async-done(((bf16[2,512,256]{2,1,0:T(8,128)(2,1)}), bf16[2,512,1024]{2,1,0:T(8,128)(2,1)}) %all-gather.2.cloned.1.call-update) | async-done | bytes 2097168 | tf_op jit(solution)/shard_map/all_gather | solution.py:48
  65.5 30.1 %while.33 = (s32[]{:T(128)}, bf16[2,512,1024]{2,1,0:T(8,128)(2,1)}, s32[8,3]{0,1:T(4,128)S(1)}, bf16[8,2,256,256]{3,2,1,0:T(8,128)(2,1)}, s32[]{:T(128)}) while((s32[]{:T(128)}, bf16[2,512,1024]{2,1,0:T(8,128)(2,1)}, s32[8,3]{0,1:T(4,128)S(1)}, bf16[8,2,256,256]{3,2,1,0:T(8,128)(2,1)}, s32[]{:T(128)}) %tuple.102), condition=%wide.while_cond.1, body=%wide.while_body.1.sunk | while | flops 2 | bytes 525429 | solution.py:54
  66.1 3.2 bitcast_dynamic-update-slice_fusion.6
  69.9 3.1 bitcast_dynamic-update-slice_fusion.6
  73.6 3.2 bitcast_dynamic-update-slice_fusion.6
  77.4 3.2 bitcast_dynamic-update-slice_fusion.6
  81.2 3.2 bitcast_dynamic-update-slice_fusion.6
  85.0 3.2 bitcast_dynamic-update-slice_fusion.6
  88.7 3.2 bitcast_dynamic-update-slice_fusion.6
  92.5 3.2 bitcast_dynamic-update-slice_fusion.6
  95.7 42.0 %while.32 = (s32[]{:T(128)}, f32[8,2,256,256]{2,3,1,0:T(8,128)}, f32[8,2,256,256]{2,3,1,0:T(8,128)}, f32[8,256,256]{2,1,0:T(8,128)}, bf16[8,2,256,256]{3,2,1,0:T...) while((s32[]{:T(128)}, f32[8,2,256,256]{2,3,1,0:T(8,128)}, ...), condition=%wide.region_2.3_spmd, body=%wide.region_0.2_spmd.sunk | while | flops 540344320 | bytes 12845209 | solution.py:81
  142.9 79.3 %all-reduce.4.cloned.1.call-done = f32[8,256,256]{2,1,0:T(8,128)} async-done(((f32[8,256,256]{2,1,0:T(8,128)}), f32[8,256,256]{2,1,0:T(8,128)}) %all-reduce.4.cloned.1.call-update) | async-done | bytes 2097168 | tf_op jit(solution)/shard_map/psum | solution.py:82
  222.2 3.8 add_multiply_fusion
  226.0 3.5 broadcast_in_dim.23.clone
  229.4 266.7 %while.34 = (s32[]{:T(128)}, f32[3,512,1024]{2,1,0:T(8,128)}, f32[2,2,256,256]{2,3,0,1:T(8,128)}, f32[256,256]{0,1:T(8,128)}, s32[8]{0:T(128)S(1)}, /*index=5*/s...) while((s32[]{:T(128)}, f32[3,512,1024]{2,1,0:T(8,128)}, ...), condition=%wide.region_8.9_spmd.clone, body=%wide.region_5.8_spmd.clone.sunk | while | flops 542769152 | bytes 35914140 | solution.py:119
  237.7 2.3 multiply_bitcast_fusion.2
  252.2 8.3 %dynamic_update_slice.23 = f32[3,512,1024]{2,1,0:T(8,128)} dynamic-update-slice(f32[3,512,1024]{2,1,0:T(8,128)} %get-tuple-element.660, f32[3,256,256]{2,1,0:T(8,128)S(1)} %copy.58, s32[]{:T(128)} %constant.100.clone.1..sunk.1, s32[]{:T(128)S(6)} %select_n.65, s32[]{:T(128)S(6)} %select_n.66) | dynamic-update-slice | bytes 1572868 | tf_op jit(solution)/shard_map/while/body/eval_jaxpr/dynamic_update_slice | solution.py:111
  267.4 2.4 select_add_fusion.2
  269.8 2.3 multiply_bitcast_fusion.2
  283.0 2.3 maximum_add_fusion.5
  285.3 7.1 %dynamic_update_slice.23 = f32[3,512,1024]{2,1,0:T(8,128)} dynamic-update-slice(f32[3,512,1024]{2,1,0:T(8,128)} %get-tuple-element.660, f32[3,256,256]{2,1,0:T(8,128)S(1)} %copy.58, s32[]{:T(128)} %constant.100.clone.1..sunk.1, s32[]{:T(128)S(6)} %select_n.65, s32[]{:T(128)S(6)} %select_n.66) | dynamic-update-slice | bytes 1572868 | tf_op jit(solution)/shard_map/while/body/eval_jaxpr/dynamic_update_slice | solution.py:111
  299.3 2.4 select_add_fusion.2
  301.6 2.3 multiply_bitcast_fusion.2
  315.0 2.3 maximum_add_fusion.5
  317.3 8.5 %dynamic_update_slice.23 = f32[3,512,1024]{2,1,0:T(8,128)} dynamic-update-slice(f32[3,512,1024]{2,1,0:T(8,128)} %get-tuple-element.660, f32[3,256,256]{2,1,0:T(8,128)S(1)} %copy.58, s32[]{:T(128)} %constant.100.clone.1..sunk.1, s32[]{:T(128)S(6)} %select_n.65, s32[]{:T(128)S(6)} %select_n.66) | dynamic-update-slice | bytes 1572868 | tf_op jit(solution)/shard_map/while/body/eval_jaxpr/dynamic_update_slice | solution.py:111
  332.7 2.4 select_add_fusion.2
  335.1 2.3 multiply_bitcast_fusion.2
  348.5 2.3 maximum_add_fusion.5
  350.8 9.4 %dynamic_update_slice.23 = f32[3,512,1024]{2,1,0:T(8,128)} dynamic-update-slice(f32[3,512,1024]{2,1,0:T(8,128)} %get-tuple-element.660, f32[3,256,256]{2,1,0:T(8,128)S(1)} %copy.58, s32[]{:T(128)} %constant.100.clone.1..sunk.1, s32[]{:T(128)S(6)} %select_n.65, s32[]{:T(128)S(6)} %select_n.66) | dynamic-update-slice | bytes 1572868 | tf_op jit(solution)/shard_map/while/body/eval_jaxpr/dynamic_update_slice | solution.py:111
  367.1 2.4 select_add_fusion.2
  369.4 2.3 multiply_bitcast_fusion.2
  382.8 2.3 maximum_add_fusion.5
  385.1 9.1 %dynamic_update_slice.23 = f32[3,512,1024]{2,1,0:T(8,128)} dynamic-update-slice(f32[3,512,1024]{2,1,0:T(8,128)} %get-tuple-element.660, f32[3,256,256]{2,1,0:T(8,128)S(1)} %copy.58, s32[]{:T(128)} %constant.100.clone.1..sunk.1, s32[]{:T(128)S(6)} %select_n.65, s32[]{:T(128)S(6)} %select_n.66) | dynamic-update-slice | bytes 1572868 | tf_op jit(solution)/shard_map/while/body/eval_jaxpr/dynamic_update_slice | solution.py:111
  401.1 2.4 select_add_fusion.2
  403.5 2.3 multiply_bitcast_fusion.2
  416.8 2.3 maximum_add_fusion.5
  419.2 9.5 %dynamic_update_slice.23 = f32[3,512,1024]{2,1,0:T(8,128)} dynamic-update-slice(f32[3,512,1024]{2,1,0:T(8,128)} %get-tuple-element.660, f32[3,256,256]{2,1,0:T(8,128)S(1)} %copy.58, s32[]{:T(128)} %constant.100.clone.1..sunk.1, s32[]{:T(128)S(6)} %select_n.65, s32[]{:T(128)S(6)} %select_n.66) | dynamic-update-slice | bytes 1572868 | tf_op jit(solution)/shard_map/while/body/eval_jaxpr/dynamic_update_slice | solution.py:111
  435.5 2.4 select_add_fusion.2
  437.9 2.3 multiply_bitcast_fusion.2
  451.2 2.3 maximum_add_fusion.5
  453.6 9.1 %dynamic_update_slice.23 = f32[3,512,1024]{2,1,0:T(8,128)} dynamic-update-slice(f32[3,512,1024]{2,1,0:T(8,128)} %get-tuple-element.660, f32[3,256,256]{2,1,0:T(8,128)S(1)} %copy.58, s32[]{:T(128)} %constant.100.clone.1..sunk.1, s32[]{:T(128)S(6)} %select_n.65, s32[]{:T(128)S(6)} %select_n.66) | dynamic-update-slice | bytes 1572868 | tf_op jit(solution)/shard_map/while/body/eval_jaxpr/dynamic_update_slice | solution.py:111
  469.5 2.4 select_add_fusion.2
  485.3 2.3 maximum_add_fusion.5
  487.6 8.5 %dynamic_update_slice.23 = f32[3,512,1024]{2,1,0:T(8,128)} dynamic-update-slice(f32[3,512,1024]{2,1,0:T(8,128)} %get-tuple-element.660, f32[3,256,256]{2,1,0:T(8,128)S(1)} %copy.58, s32[]{:T(128)} %constant.100.clone.1..sunk.1, s32[]{:T(128)S(6)} %select_n.65, s32[]{:T(128)S(6)} %select_n.66) | dynamic-update-slice | bytes 1572868 | tf_op jit(solution)/shard_map/while/body/eval_jaxpr/dynamic_update_slice | solution.py:111
  498.3 5.1 collective-permute-start.1
  505.5 4.9 convert_add_fusion
  510.3 61.3 %all-reduce.6.cloned.1.call-done = (f32[2,2,256,256]{3,2,1,0:T(8,128)}, f32[256,256]{0,1:T(8,128)}) async-done(((f32[2,2,256,256]{3,2,1,0:T(8,128)}, f32[256,256]{0,1:T(8,128)}), (f32[2,2,256,256]{3,2,1,0:T(8,128)}, f32[256,256]{0,1:T(8,128)})) %all-reduce.6.cloned.1.call-update) | async-done | bytes 1310736 | tf_op jit(solution)/shard_map/psum | solution.py:129
  575.0 58.3 %reduce-scatter.2.cloned.1.call-done = f32[3,256,256]{2,1,0:T(8,128)} async-done(((f32[3,256,1024]{2,1,0:T(8,128)}), f32[3,256,256]{2,1,0:T(8,128)}) %reduce-scatter.2.cloned.1.call-update) | async-done | bytes 786448 | tf_op jit(solution)/shard_map/reduce_scatter | solution.py:126
  (311 shorter events, 189.0 us)
Async XLA Ops:
  7.2 5.7 copy-start.8
  7.2 58.4 %all-gather.2.cloned.1.call-start = ((), (), s32[]{:S(2)}) async-start(), calls=%async_computation.1 | async-start | bytes 2621440 | tf_op jit(solution)/shard_map/all_gather | solution.py:48
  8.3 8.3 %copy-start.6 = (f32[2,2,256,256]{3,2,1,0:T(8,128)S(1)}, f32[2,2,256,256]{3,2,1,0:T(8,128)}, u32[]{:S(2)}) copy-start(f32[2,2,256,256]{3,2,1,0:T(8,128)} %param.14) | copy-start | bytes 3145732
  8.3 3.6 collective-permute-start
  12.7 209.4 %all-reduce.4.cloned.1.call-start = ((), (), s32[]{:S(2)}) async-start(), calls=%async_computation.2 | async-start | bytes 4194304 | tf_op jit(solution)/shard_map/psum | solution.py:82
  137.6 1.0 copy-start.5
  137.6 2.0 copy-start.4
  137.7 84.5 %copy-start.7 = (bf16[8,256,256]{2,1,0:T(8,128)(2,1)S(1)}, bf16[8,256,256]{2,1,0:T(8,128)(2,1)}, u32[]{:S(2)}) copy-start(bf16[8,256,256]{2,1,0:T(8,128)(2,1)} %param.15) | copy-start | bytes 3145732
  137.7 434.0 %all-reduce.6.cloned.1.call-start = ((), (), s32[]{:S(2)}) async-start(), calls=%async_computation.4 | async-start | bytes 2621440 | tf_op jit(solution)/shard_map/psum | solution.py:129
  248.5 1.5 copy-start.2
  250.0 1.0 copy-start
  280.4 1.5 copy-start.2
  282.0 1.0 copy-start
  312.4 1.5 copy-start.2
  314.0 1.0 copy-start
  345.9 1.5 copy-start.2
  347.4 1.0 copy-start
  380.2 1.5 copy-start.2
  381.8 1.0 copy-start
  414.3 1.5 copy-start.2
  415.8 1.0 copy-start
  448.7 1.5 copy-start.2
  450.2 1.0 copy-start
  482.7 1.5 copy-start.2
  484.2 1.0 copy-start
  496.1 7.3 %copy-start.1 = (f32[2,2,256,256]{2,3,0,1:T(8,128)S(1)}, f32[2,2,256,256]{2,3,0,1:T(8,128)}, u32[]{:S(2)}) copy-start(f32[2,2,256,256]{2,3,0,1:T(8,128)} %get-tuple-element.159) | copy-start | bytes 3145732
  498.3 7.1 %collective-permute-start.1 = (bf16[3,256,1024]{2,1,0:T(8,128)(2,1)S(1)}, bf16[3,256,1024]{2,1,0:T(8,128)(2,1)}, u32[]{:S(2)}, u32[]{:S(2)}) collective-permute-start(bf16[3,256,1024]{2,1,0:T(8,128)(2,1)S(1)} %slice.165), channel_id=1, source_target_pairs={{0,4},{4,8},{8,12},{12,16},{16,20},{20,24},{24,28},{1,5},{5,9},{9,... | collective-permute-start | bytes 4718600 | tf_op jit(solution)/shard_map/ppermute | solution.py:15
  504.8 128.6 %reduce-scatter.2.cloned.1.call-start = ((), (), s32[]{:S(2)}) async-start(), calls=%async_computation.3 | async-start | bytes 3932160 | tf_op jit(solution)/shard_map/reduce_scatter | solution.py:126
  510.3 124.0 %copy-start.3 = (f32[2,256,256]{2,1,0:T(8,128)S(1)}, f32[2,256,256]{2,1,0:T(8,128)}, u32[]{:S(2)}) copy-start(f32[2,256,256]{2,1,0:T(8,128)} %param.13) | copy-start | bytes 1572868
Sparse Core Ops, SparseCore 0:
  12.8 52.6 all-gather.1
  137.8 84.3 all-reduce.3
  504.9 66.6 all-reduce.5
  573.8 59.5 reduce-scatter.1
where the time goes:
time: 649 us; the launch traced here: 643 us
  waiting for transfers between devices  249 us (38%)
  local copies, waits for them, and re-layouts  184 us (28%)
  other arithmetic  134 us (21%)
  loops' own time  31.6 us (5%)
  matrix products  22.2 us (3%)
  between operations  14.7 us (2%)
  starting transfers between devices  6.7 us (1%)
    psum x1, waiting for transfers between devices, shards(): intensity = lax.psum(local_power, 'tile')  79.3 us
    dynamic_update_slice x16, local copies, waits for them, and re-layouts, accumulate(): lax.dynamic_update_slice(buffer, region + numer, (zero_index, row_at, col...  71.5 us
    psum x1, waiting for transfers between devices, shards(): grad_total, weight_total = lax.psum((grad_sum, weight_sum), 'scan')  61.3 us
    reduce_scatter x1, waiting for transfers between devices, shards(): totals = lax.psum_scatter(own_rows, 'tile', scatter_dimension=2, tiled=True)  58.3 us
    all_gather x1, waiting for transfers between devices, shards(): band_all = lax.all_gather(extended, 'tile', axis=2, tiled=True)  47.6 us
    add x16, other arithmetic, accumulate(): return ((buffer, grad_sum + grads, weight_sum + live * weight), None)  35.4 us
    another operation x1, loops' own time, shards(): lax.scan(accumulate, init, (far_re, far_im, factor, windows, live_mask, r...  31.4 us
    gather x24, local copies, waits for them, and re-layouts  30.1 us
  transfers between devices with their start and end apart: 6, of which 6 were waited for; matrix products, arithmetic and copies ran while one was open for 3% of the time, Pallas kernels for 0%

commit v1 on v0

v1 whole, which is shorter than its diff:
```python
import math

import jax
import jax.numpy as jnp
import numpy as np
from jax import lax
from jax.experimental import pallas as pl
from jax.experimental.pallas import tpu as pltpu
from jax.sharding import PartitionSpec as P


damping = 1.0
amp_floor = 0.5
f32 = jnp.float32
bf16 = jnp.bfloat16


def shifted(value, axis, steps):
    count = lax.axis_size(axis)
    pairs = [(i, i + steps) for i in range(max(0, -steps), min(count, count - steps))]
    return lax.ppermute(value, axis, pairs)


def rotated(value, axis, steps):
    count = lax.axis_size(axis)
    return lax.ppermute(value, axis, [(i, (i + steps) % count) for i in range(count)])


def swapped(value, axis, mask):
    pairs = [(i, i ^ mask) for i in range(lax.axis_size(axis))]
    return lax.ppermute(value, axis, pairs)


def dft_tables(width):
    index = np.arange(width, dtype=np.int32)
    angle = (index[:, None] * index[None, :] % width).astype(np.float32) * np.float32(
        2.0 * math.pi / width
    )
    scale = np.float32(1.0 / math.sqrt(width))
    real = jnp.asarray(np.cos(angle) * scale, bf16)
    imag = jnp.asarray(-np.sin(angle) * scale, bf16)
    plus = jnp.block([[real, imag], [-imag, real]])
    minus = jnp.block([[real, -imag], [imag, real]])
    return plus, minus


def dot(a, b):
    return jnp.dot(a, b, preferred_element_type=f32)


def add_window(ref, lead, value, row, col, col_limit):
    width = value.shape[0]
    row_at = pl.multiple_of(row // 8 * 8, 8)
    col_at = pl.multiple_of(jnp.minimum(col // 128 * 128, col_limit - width - 128), 128)
    value = jnp.concatenate([value, jnp.zeros((8, width), f32)], 0)
    value = pltpu.roll(value, row - row_at, 0)
    value = jnp.concatenate([value, jnp.zeros((width + 8, 128), f32)], 1)
    value = pltpu.roll(value, col - col_at, 1)
    if lead is None:
        ref[pl.ds(row_at, width + 8), pl.ds(col_at, width + 128)] += value
    else:
        ref[lead, pl.ds(row_at, width + 8), pl.ds(col_at, width + 128)] += value


def cut_window(ref, lead, row, col, width, col_limit):
    row_at = pl.multiple_of(row // 16 * 16, 16)
    col_at = pl.multiple_of(jnp.minimum(col // 128 * 128, col_limit - width - 128), 128)
    value = ref[lead, pl.ds(row_at, width + 16), pl.ds(col_at, width + 128)].astype(f32)
    value = pltpu.roll(value, width + 128 - (col - col_at), 1)[:, :width]
    return pltpu.roll(value, width + 16 - (row - row_at), 0)[:width]


def main_kernel(tiles, slots, modes, width, band, spread, part):
    cols = tiles * band

    def body(*refs):
        meta = refs[0]
        blocks = refs[1 : 1 + tiles]
        rims = refs[1 + tiles : 1 + 2 * tiles]
        (
            own_probe,
            first_a,
            first_b,
            second_a,
            second_b,
            amp_ref,
            plus_ref,
            minus_ref,
            main_out,
            rim_out,
            power_out,
            *rest,
        ) = refs[1 + 2 * tiles :]
        odd_out = rest[0]
        even_out = rest[1]
        band_ref, probe, far, half, buffer, grads, win, fac, num, weight = rest[2:]
        scan_at = meta[0]
        tile_at = meta[1]
        local = modes // tiles
        for d in range(tiles):
            source = (tile_at - d + tiles) % tiles
            at = pl.multiple_of(source * band, band)
            for ch in range(2):
                band_ref[ch, 0:band, pl.ds(at, band)] = blocks[d][ch]
                band_ref[ch, band : 2 * band, pl.ds(at, band)] = rims[d][ch]
        for m in range(local):
            probe[tile_at * local + m] = own_probe[m]
        for k in range(spread // 2):
            for start, masks, pair in (
                (0, (2, 4), (first_a, first_b)),
                (local // 2, (4, 2), (second_a, second_b)),
            ):
                offset = (k & 1) * masks[0] + (k >> 1) * masks[1]
                for flip in range(2):
                    at = pl.multiple_of(((scan_at % spread) ^ (offset + flip)) * part, part)
                    for d in range(1, tiles):
                        source = (tile_at - d + tiles) % tiles
                        for m in range(local // 2):
                            for ch in range(2):
                                probe[source * local + start + m, ch, pl.ds(at, part), :] = pair[
                                    flip
                                ][k, d - 1, m, ch]
        power = jnp.zeros((width, width), f32)
        for m in range(modes):
            power = power + probe[m, 0] * probe[m, 0] + probe[m, 1] * probe[m, 1]
        power_out[...] = power
        buffer[...] = jnp.zeros_like(buffer)
        grads[...] = jnp.zeros_like(grads)
        weight[...] = jnp.zeros_like(weight)

        def one_slot(k, carry):
            slot = tile_at + tiles * k
            row = meta[2 + 2 * slot] - scan_at * band
            col = meta[3 + 2 * slot]
            live = (slot < meta[2 + 2 * slots * tiles]).astype(f32)
            for ch in range(2):
                win[ch] = cut_window(band_ref, ch, row, col, width, cols)
            weight[...] += live * (win[0] * win[0] + win[1] * win[1])
            fac[...] = jnp.zeros_like(fac)
            for m in range(modes):
                er = (probe[m, 0] * win[0] - probe[m, 1] * win[1]).astype(bf16)
                ei = (probe[m, 0] * win[1] + probe[m, 1] * win[0]).astype(bf16)
                h = dot(jnp.concatenate([er, ei], 1), plus_ref[...])
                half[m % 2, 0:width] = h[:, :width].astype(bf16)
                half[m % 2, width : 2 * width] = h[:, width:].astype(bf16)
                z = dot(minus_ref[...], half[m % 2])
                far[m] = z
                fac[...] += z[:width] * z[:width] + z[width:] * z[width:]
            fac[...] = live * (
                amp_ref[slot].astype(f32) / jnp.maximum(jnp.sqrt(fac[...]), amp_floor) - 1.0
            )
            num[...] = jnp.zeros_like(num)
            for m in range(modes):
                cr = (fac[...] * far[m, :width]).astype(bf16)
                ci = (fac[...] * far[m, width:]).astype(bf16)
                h = dot(jnp.concatenate([cr, ci], 1), minus_ref[...])
                half[m % 2, 0:width] = h[:, :width].astype(bf16)
                half[m % 2, width : 2 * width] = h[:, width:].astype(bf16)
                z = dot(plus_ref[...], half[m % 2])
                nr = z[:width]
                ni = z[width:]
                num[0] += probe[m, 0] * nr + probe[m, 1] * ni
                num[1] += probe[m, 0] * ni - probe[m, 1] * nr
                grads[2 * m] += win[0] * nr + win[1] * ni
                grads[2 * m + 1] += win[0] * ni - win[1] * nr
            for ch in range(2):
                add_window(buffer, ch, num[ch], row, col, cols)
            return carry

        lax.fori_loop(0, slots, one_slot, 0)
        for d in range(tiles):
            for ch in range(2):
                at = pl.multiple_of((tile_at + d) % tiles * band, band)
                main_out[d, ch] = buffer[ch, 0:band, pl.ds(at, band)].astype(bf16)
                rim_out[d, ch] = buffer[ch, band : 2 * band, pl.ds(at, band)].astype(bf16)
        for k in range(spread):
            at = pl.multiple_of(((scan_at % spread) ^ k) * part, part)
            out = odd_out if k % 2 else even_out
            for d in range(tiles):
                first = (tile_at + d) % tiles * local * 2
                for ch in range(2 * local):
                    value = grads[first + ch, pl.ds(at, part)]
                    out[k // 2, d * 2 * local + ch] = value.astype(out.dtype)
            out[k // 2, 2 * modes] = weight[pl.ds(at, part)].astype(out.dtype)

    return body


def illum_kernel(count, width, band):
    def body(meta, above, power, out, buffer):
        buffer[...] = jnp.zeros_like(buffer)
        corner_row = width - meta[0] * band
        corner_col = width - meta[1] * band

        def one(k, carry):
            mine = k < count
            slot = jnp.where(mine, k, k - count)
            live = slot < jnp.where(mine, meta[2 + 2 * count], above[2 * count])
            row = jnp.where(mine, meta[2 + 2 * slot], above[2 * slot]) + corner_row
            col = jnp.where(mine, meta[3 + 2 * slot], above[2 * slot + 1]) + corner_col

            @pl.when(live & (col > 0) & (col < width + band))
            def _():
                add_window(buffer, None, power[...], row, col, 2 * width + band)

            return carry

        lax.fori_loop(0, 2 * count, one, 0)
        out[...] = buffer[width : width + band, width : width + band]

    return body


def join_kernel(local, spread, part):
    def body(meta, steps, mates, out):
        for k in range(spread):
            at = pl.multiple_of(((meta[0] % spread) ^ k) * part, part)
            for m in range(local):
                for ch in range(2):
                    pick = mates if k % 2 else steps
                    out[m, ch, pl.ds(at, part), :] = pick[k // 2, 2 * m + ch]

    return body


def update(object_field, probe_modes, amplitudes, positions, counts):
    scans = lax.axis_size("scan")
    tiles = lax.axis_size("tile")
    scan_at = lax.axis_index("scan")
    tile_at = lax.axis_index("tile")
    slot_count, width = amplitudes.shape[:2]
    local = probe_modes.shape[0]
    modes = local * tiles
    band = object_field.shape[1]
    slots = slot_count // tiles
    spread = min(scans, 8)
    part = width // spread
    ids = jnp.stack([scan_at, tile_at]).astype(jnp.int32)
    spots = jnp.concatenate([positions.reshape(-1), counts])
    meta = jnp.concatenate([ids, spots])
    above = shifted(spots, "scan", 1)

    piece = lax.dynamic_slice_in_dim(probe_modes, (scan_at % spread) * part, part, 2)
    pieces = jnp.stack([rotated(piece, "tile", d) for d in range(1, tiles)])[None]
    first = pieces[:, :, : local // 2]
    second = pieces[:, :, local // 2 :]
    first = jnp.concatenate([first, swapped(first, "scan", 2)])
    second = jnp.concatenate([second, swapped(second, "scan", 4)])
    first = jnp.concatenate([first, swapped(first, "scan", 4)])
    second = jnp.concatenate([second, swapped(second, "scan", 2)])
    first_mate = swapped(first, "scan", 1)
    second_mate = swapped(second, "scan", 1)

    low = object_field.astype(bf16)
    blocks = [low] + [rotated(low, "tile", d) for d in range(1, tiles)]
    rims = [shifted(b, "scan", -1) for b in blocks]

    plus, minus = dft_tables(width)
    vmem = pl.BlockSpec(memory_space=pltpu.VMEM)
    smem = pl.BlockSpec(memory_space=pltpu.SMEM)
    main, rim, power, odd, even = pl.pallas_call(
        main_kernel(tiles, slots, modes, width, band, spread, part),
        out_shape=(
            jax.ShapeDtypeStruct((tiles, 2, band, band), bf16),
            jax.ShapeDtypeStruct((tiles, 2, band, band), bf16),
            jax.ShapeDtypeStruct((width, width), f32),
            jax.ShapeDtypeStruct((spread // 2, 2 * modes + 1, part, width), bf16),
            jax.ShapeDtypeStruct((spread // 2, 2 * modes + 1, part, width), f32),
        ),
        in_specs=[smem] + [vmem] * (2 * tiles + 8),
        out_specs=(vmem,) * 5,
        scratch_shapes=[
            pltpu.VMEM((2, 2 * band, tiles * band), bf16),
            pltpu.VMEM((modes, 2, width, width), f32),
            pltpu.VMEM((modes, 2 * width, width), f32),
            pltpu.VMEM((2, 2 * width, width), bf16),
            pltpu.VMEM((2, 2 * band, tiles * band), f32),
            pltpu.VMEM((2 * modes, width, width), f32),
            pltpu.VMEM((2, width, width), f32),
            pltpu.VMEM((width, width), f32),
            pltpu.VMEM((2, width, width), f32),
            pltpu.VMEM((width, width), f32),
        ],
        name="update",
    )(
        meta,
        *blocks,
        *rims,
        probe_modes,
        first,
        first_mate,
        second,
        second_mate,
        amplitudes,
        plus,
        minus,
    )

    share = main.astype(f32) + shifted(rim, "scan", 1).astype(f32)
    totals = share[0]
    for d in range(1, tiles):
        totals = totals + rotated(share[d].astype(bf16), "tile", d).astype(f32)

    illumination = pl.pallas_call(
        illum_kernel(slot_count, width, band),
        out_shape=jax.ShapeDtypeStruct((band, band), f32),
        in_specs=[smem] * 2 + [vmem],
        out_specs=vmem,
        scratch_shapes=[pltpu.VMEM((2 * width + band, 2 * width + band), f32)],
        name="illumination",
    )(meta, above, power)
    new_object = object_field + totals / (illumination + damping)

    even = even + swapped(odd, "scan", 1).astype(f32)
    total = even[0]
    for k in range(1, spread // 2):
        total = total + swapped(even[k].astype(bf16), "scan", 2 * k).astype(f32)
    mask = spread
    while mask < scans:
        total = total + swapped(total, "scan", mask)
        mask *= 2
    step = None
    for d in range(tiles):
        share = jnp.concatenate([total[2 * local * d : 2 * local * (d + 1)], total[2 * modes :]])
        share = rotated(share, "tile", d) if d else share
        step = share if step is None else step + share
    step = step[: 2 * local] / (step[2 * local] + damping)
    steps = [step] + [swapped(step, "scan", 2 * k) for k in range(1, spread // 2)]
    steps = jnp.stack(steps)
    mates = swapped(steps, "scan", 1)
    probe_step = pl.pallas_call(
        join_kernel(local, spread, part),
        out_shape=jax.ShapeDtypeStruct(probe_modes.shape, f32),
        in_specs=[smem, vmem, vmem],
        out_specs=vmem,
        name="join",
    )(meta, steps, mates)
    return (new_object, probe_step)


def solution(mesh):
    placed = (
        P(None, "scan", "tile"),
        P("tile", None, None, None),
        P("scan", None, None),
        P("scan", None),
        P("scan"),
    )
    return jax.shard_map(
        update,
        mesh=mesh,
        in_specs=placed,
        out_specs=(P(None, "scan", "tile"), P("tile", None, None, None)),
        check_vma=False,
    )
```

time: 649 us -> 175 us (0.27)
  local copies, waits for them, and re-layouts: 184 us -> 3.56 us
  waiting for transfers between devices: 249 us -> 80.1 us
  other arithmetic: 134 us -> 4.71 us
  starting transfers between devices: 6.7 us -> 57.4 us
  loops' own time: 31.6 us -> 0 us
  Pallas kernels: 0 us -> 26.9 us
  matrix products: 22.2 us -> 0 us
  between operations: 14.7 us -> 1.7 us
    psum x2 -> x0, waiting for transfers between devices: 141 us -> none  [the longest x1 79.3 us: shards(): intensity = lax.psum(local_power, 'tile')]
    dynamic_update_slice x32 -> x0, local copies, waits for them, and re-layouts: 78.3 us -> none  [the longest x16 71.5 us: accumulate(): lax.dynamic_update_slice(buffer, region + numer, (zero_index, row_at, col...]
    ppermute x2 -> x32, waiting for transfers between devices: 2.75 us -> 80.1 us  [the longest x12 52.7 us: rotated(): lax.ppermute(value, axis, [(i, (i + steps) % count) for i in range(count)])]
    reduce_scatter x1 -> x0, waiting for transfers between devices: 58.3 us -> none  [shards(): totals = lax.psum_scatter(own_rows, 'tile', scatter_dimension=2, tiled=True)]
    ppermute x2 -> x32, starting transfers between devices: 6.54 us -> 57.4 us  [the longest x14 28.8 us: swapped(): return lax.ppermute(value, axis, pairs)]
    all_gather x1 -> x0, waiting for transfers between devices: 47.6 us -> none  [shards(): band_all = lax.all_gather(extended, 'tile', axis=2, tiled=True)]
    add x27 -> x4, other arithmetic: 44 us -> 1.22 us  [the longest x2 1.01 us: update(): new_object = object_field + totals / (illumination + damping)]
    dynamic_slice x64 -> x1, local copies, waits for them, and re-layouts: 42.9 us -> 0.97 us  [update(): lax.dynamic_slice_in_dim(probe_modes, scan_at % spread * part, part, 2)]
  transfers between devices with their start and end apart: 6 -> 32, of which waited for: 6 -> 18; matrix products, arithmetic and copies ran while one was open for 3% -> 3% of each run, Pallas kernels for 0% -> 1%
where the time goes in v1:
time: 175 us; the launch traced here: 174 us
  waiting for transfers between devices  80.1 us (46%)
  starting transfers between devices  57.4 us (33%)
  Pallas kernels  26.9 us (15%)
  other arithmetic  4.71 us (3%)
  local copies, waits for them, and re-layouts  3.56 us (2%)
    ppermute x12, waiting for transfers between devices, rotated(): lax.ppermute(value, axis, [(i, (i + steps) % count) for i in range(count)])  52.7 us
    ppermute x14, starting transfers between devices, swapped(): return lax.ppermute(value, axis, pairs)  28.8 us
    ppermute x14, waiting for transfers between devices, swapped(): return lax.ppermute(value, axis, pairs)  25.2 us
    pallas_call x1, Pallas kernels, update(): pl.pallas_call(main_kernel(tiles, slots, modes, width, band, spread, part...  22.3 us
    ppermute x12, starting transfers between devices, rotated(): lax.ppermute(value, axis, [(i, (i + steps) % count) for i in range(count)])  17 us
    ppermute x6, starting transfers between devices, shifted(): return lax.ppermute(value, axis, pairs)  11.6 us
  transfers between devices with their start and end apart: 32, of which 18 were waited for; matrix products, arithmetic and copies ran while one was open for 3% of the time, Pallas kernels for 1%

profile of v1, /device:TPU:0, one launch (start us, length us, event | category | flops | bytes accessed | tf_op | source)
XLA Modules:
  0.0 174.4 jit_solution(14817872711486774682)
XLA Ops:
  0.7 1.0 constant_dynamic-slice_fusion
  1.6 5.1 %collective-permute-start.9 = (f32[2,2,32,256]{3,2,1,0:T(8,128)S(1)}, f32[2,2,32,256]{3,2,1,0:T(8,128)S(1)}, u32[]{:S(2)}, u32[]{:S(2)}) collective-permute-start(f32[2,2,32,256]{3,2,1,0:T(8,128)S(1)} %constant_dynamic-slice_fusion), channel_id=1, source_target_pairs={{0,3},{1,0},{2,1},{3,2},{4,7},{5,4},{6,5},{7,6},{8,11},{9,8},{10,9... | collective-permute-start | bytes 393224 | tf_op jit(solution)/shard_map/ppermute | solution.py:26
  6.8 1.0 collective-permute-start.7
  7.8 2.9 %collective-permute-done.9 = f32[2,2,32,256]{3,2,1,0:T(8,128)S(1)} collective-permute-done((f32[2,2,32,256]{3,2,1,0:T(8,128)S(1)}, f32[2,2,32,256]{3,2,1,0:T(8,128)S(1)}, u32[]{:S(2)}, u32[]{:S(2)}) %collective-permute-start.9) | collective-permute-done | bytes 131104 | tf_op jit(solution)/shard_map/ppermute | solution.py:26
  10.7 7.3 %collective-permute-done.8 = f32[2,2,32,256]{3,2,1,0:T(8,128)S(1)} collective-permute-done((f32[2,2,32,256]{3,2,1,0:T(8,128)S(1)}, f32[2,2,32,256]{3,2,1,0:T(8,128)S(1)}, u32[]{:S(2)}, u32[]{:S(2)}) %collective-permute-start.8) | collective-permute-done | bytes 131104 | tf_op jit(solution)/shard_map/ppermute | solution.py:26
  18.1 1.6 collective-permute-start.10
  19.6 1.5 collective-permute-start.13
  21.1 3.2 %collective-permute-done.10 = f32[1,3,1,2,32,256]{5,4,3,2,1,0:T(8,128)S(1)} collective-permute-done((f32[1,3,1,2,32,256]{5,4,3,2,1,0:T(8,128)S(1)}, f32[1,3,1,2,32,256]{5,4,3,2,1,0:T(8,128)S(1)}, u32[]{:S(2)}, u32[]{:S(2)}) %collective-permute-start.10) | collective-permute-done | bytes 196640 | tf_op jit(solution)/shard_map/ppermute | solution.py:31
  24.4 1.6 collective-permute-start.11
  26.0 1.6 collective-permute-start.14
  27.6 1.3 collective-permute-start.3
  28.9 5.1 %collective-permute-done.11 = f32[2,3,1,2,32,256]{5,4,3,2,1,0:T(8,128)S(1)} collective-permute-done((f32[2,3,1,2,32,256]{5,4,3,2,1,0:T(8,128)S(1)}, f32[2,3,1,2,32,256]{5,4,3,2,1,0:T(8,128)S(1)}, u32[]{:S(2)}, u32[]{:S(2)}) %collective-permute-start.11) | collective-permute-done | bytes 393248 | tf_op jit(solution)/shard_map/ppermute | solution.py:31
  34.2 1.2 collective-permute-done.14
  35.5 0.9 collective-permute-start.2
  36.4 1.6 collective-permute-start.1
  38.0 1.9 %collective-permute-start = (bf16[2,256,256]{2,1,0:T(8,128)(2,1)S(1)}, bf16[2,256,256]{2,1,0:T(8,128)(2,1)}, u32[]{:S(2)}, u32[]{:S(2)}) collective-permute-start(bf16[2,256,256]{2,1,0:T(8,128)(2,1)S(1)} %convert_element_type.54.refs_1_), channel_id=1, source_target_pairs={{0,1},{1,2},{2,3},{3,0},{4,5},{5,6},{6,7},{7,4},{8,9},{9,10},{10,1... | collective-permute-start | bytes 786440 | tf_op jit(solution)/shard_map/ppermute | solution.py:26
  40.0 4.3 %collective-permute-done.2.refs_4_ = bf16[2,256,256]{2,1,0:T(8,128)(2,1)} collective-permute-done((bf16[2,256,256]{2,1,0:T(8,128)(2,1)S(1)}, bf16[2,256,256]{2,1,0:T(8,128)(2,1)}, u32[]{:S(2)}, u32[]{:S(2)}) %collective-permute-start.2) | collective-permute-done | bytes 262176 | tf_op jit(solution)/shard_map/ppermute | solution.py:26
  44.3 1.3 collective-permute-start.6
  45.6 16.2 %collective-permute-done.1.refs_3_ = bf16[2,256,256]{2,1,0:T(8,128)(2,1)} collective-permute-done((bf16[2,256,256]{2,1,0:T(8,128)(2,1)S(1)}, bf16[2,256,256]{2,1,0:T(8,128)(2,1)}, u32[]{:S(2)}, u32[]{:S(2)}) %collective-permute-start.1) | collective-permute-done | bytes 262176 | tf_op jit(solution)/shard_map/ppermute | solution.py:26
  61.8 1.3 collective-permute-start.5
  63.1 1.3 collective-permute-start.4
  65.9 1.6 collective-permute-done.4.refs_6_
  67.6 0.8 copy-done.7
  68.4 22.3 %update.1 = (bf16[4,2,256,256]{3,2,1,0:T(8,128)(2,1)}, bf16[4,2,256,256]{3,2,1,0:T(8,128)(2,1)}, f32[256,256]{1,0:T(8,128)}, bf16[4,17,32,256]{3,2,1,0:T(8,128)(2,1)}, f32[4,17,32,256]{3,2,1,0:T(8,128)}) custom-call(s32[19]{0:T(128)} %pad_add_fusion.refs_0_.meta, bf16[2,256,256]{2,1,0:T(8,128)(2,1)} %copy-done.5, ...), custom_call_target="tpu_custom_call" | custom-call | tf_op jit(solution)/shard_map/update/pallas_call | solution.py:261
  90.7 5.0 %collective-permute-start.21 = (bf16[4,17,32,256]{3,2,1,0:T(8,128)(2,1)}, bf16[4,17,32,256]{3,2,1,0:T(8,128)(2,1)S(1)}, u32[]{:S(2)}, u32[]{:S(2)}) collective-permute-start(bf16[4,17,32,256]{3,2,1,0:T(8,128)(2,1)} %get-tuple-element.11), channel_id=1, source_target_pairs={{0,4},{4,0},{8,12},{12,8},{16,20},{20,16},{24,28},{28,24},{1,5},{5... | collective-permute-start | bytes 3342344 | tf_op jit(solution)/shard_map/ppermute | solution.py:31
  95.6 2.0 %collective-permute-start.16 = (bf16[4,2,256,256]{3,2,1,0:T(8,128)(2,1)}, bf16[4,2,256,256]{3,2,1,0:T(8,128)(2,1)S(1)}, u32[]{:S(2)}, u32[]{:S(2)}) collective-permute-start(bf16[4,2,256,256]{3,2,1,0:T(8,128)(2,1)} %get-tuple-element.8), channel_id=1, source_target_pairs={{0,4},{4,8},{8,12},{12,16},{16,20},{20,24},{24,28},{1,5},{5,9},{9,... | collective-permute-start | bytes 3145736 | tf_op jit(solution)/shard_map/ppermute | solution.py:21
  97.7 4.5 %collective-permute-start.20 = (s32[17]{0:T(128)S(1)}, s32[17]{0:T(128)S(1)}, u32[]{:S(2)}, u32[]{:S(2)}) collective-permute-start(s32[17]{0:T(128)S(1)} %pad_add_fusion.1), channel_id=1, source_target_pairs={{0,4},{4,8},{8,12},{12,16},{16,20},{20,24},{24,28},{1,5},{5,9},{9,... | collective-permute-start | bytes 212 | tf_op jit(solution)/shard_map/ppermute | solution.py:21
  103.4 2.4 %illumination.1 = f32[256,256]{1,0:T(8,128)} custom-call(s32[19]{0:T(128)} %pad_add_fusion.refs_0_.meta, s32[17]{0:T(128)} %copy-done.11, f32[256,256]{1,0:T(8,128)} %get-tuple-element.9.power), custom_call_target="tpu_custom_call" | custom-call | tf_op jit(solution)/shard_map/illumination/pallas_call | solution.py:304
  105.8 2.1 %fusion.13 = (bf16[4,17,32,256]{3,2,1,0:T(8,128)(2,1)S(1)}, f32[4,17,32,256]{3,2,1,0:T(8,128)S(1)}) fusion(f32[4,17,32,256]{3,2,1,0:T(8,128)} %get-tuple-element.10, bf16[4,17,32,256]{3,2,1,0:T(8,128)(2,1)S(1)} %collective-permute-done.21), kind=kLoop, calls=%fused_computation.38 | loop fusion | flops 1671168 | bytes 6684672 | tf_op jit(solution)/shard_map/convert.2
  108.0 11.9 %collective-permute-start.22 = (bf16[17,32,256]{2,1,0:T(8,128)(2,1)S(1)}, bf16[17,32,256]{2,1,0:T(8,128)(2,1)S(1)}, u32[]{:S(2)}, u32[]{:S(2)}) collective-permute-start(bf16[17,32,256]{2,1,0:T(8,128)(2,1)S(1)} %get-tuple-element.16), channel_id=1, source_target_pairs={{0,8},{4,12},{8,0},{12,4},{16,24},{20,28},{24,16},{28,20},{1,9},{5... | collective-permute-start | bytes 835592 | tf_op jit(solution)/shard_map/ppermute | solution.py:31
  119.9 1.3 collective-permute-start.24
  121.7 5.6 %collective-permute-done.22 = bf16[17,32,256]{2,1,0:T(8,128)(2,1)S(1)} collective-permute-done((bf16[17,32,256]{2,1,0:T(8,128)(2,1)S(1)}, bf16[17,32,256]{2,1,0:T(8,128)(2,1)S(1)}, u32[]{:S(2)}, u32[]{:S(2)}) %collective-permute-start.22) | collective-permute-done | bytes 278560 | tf_op jit(solution)/shard_map/ppermute | solution.py:31
  127.4 2.8 %collective-permute-done.24 = bf16[17,32,256]{2,1,0:T(8,128)(2,1)S(1)} collective-permute-done((bf16[17,32,256]{2,1,0:T(8,128)(2,1)S(1)}, bf16[17,32,256]{2,1,0:T(8,128)(2,1)S(1)}, u32[]{:S(2)}, u32[]{:S(2)}) %collective-permute-start.24) | collective-permute-done | bytes 278560 | tf_op jit(solution)/shard_map/ppermute | solution.py:31
  130.2 2.9 %collective-permute-done.23 = bf16[17,32,256]{2,1,0:T(8,128)(2,1)S(1)} collective-permute-done((bf16[17,32,256]{2,1,0:T(8,128)(2,1)S(1)}, bf16[17,32,256]{2,1,0:T(8,128)(2,1)S(1)}, u32[]{:S(2)}, u32[]{:S(2)}) %collective-permute-start.23) | collective-permute-done | bytes 278560 | tf_op jit(solution)/shard_map/ppermute | solution.py:31
  133.5 2.1 %collective-permute-start.25 = (f32[5,32,256]{2,1,0:T(8,128)S(1)}, f32[5,32,256]{2,1,0:T(8,128)S(1)}, u32[]{:S(2)}, u32[]{:S(2)}) collective-permute-start(f32[5,32,256]{2,1,0:T(8,128)S(1)} %get-tuple-element.27), channel_id=1, source_target_pairs={{0,1},{1,2},{2,3},{3,0},{4,5},{5,6},{6,7},{7,4},{8,9},{9,10},{10,1... | collective-permute-start | bytes 491528 | tf_op jit(solution)/shard_map/ppermute | solution.py:26
  136.0 2.0 %collective-permute-start.17 = (bf16[2,256,256]{2,1,0:T(8,128)(2,1)S(1)}, bf16[2,256,256]{2,1,0:T(8,128)(2,1)S(1)}, u32[]{:S(2)}, u32[]{:S(2)}) collective-permute-start(bf16[2,256,256]{2,1,0:T(8,128)(2,1)S(1)} %get-tuple-element.19), channel_id=1, source_target_pairs={{0,1},{1,2},{2,3},{3,0},{4,5},{5,6},{6,7},{7,4},{8,9},{9,10},{10,1... | collective-permute-start | bytes 786440 | tf_op jit(solution)/shard_map/ppermute | solution.py:26
  138.0 1.9 %collective-permute-start.19 = (bf16[2,256,256]{2,1,0:T(8,128)(2,1)S(1)}, bf16[2,256,256]{2,1,0:T(8,128)(2,1)S(1)}, u32[]{:S(2)}, u32[]{:S(2)}) collective-permute-start(bf16[2,256,256]{2,1,0:T(8,128)(2,1)S(1)} %get-tuple-element.20), channel_id=1, source_target_pairs={{0,3},{1,0},{2,1},{3,2},{4,7},{5,4},{6,5},{7,6},{8,11},{9,8},{10,9... | collective-permute-start | bytes 786440 | tf_op jit(solution)/shard_map/ppermute | solution.py:26
  139.9 5.7 %collective-permute-done.27 = f32[5,32,256]{2,1,0:T(8,128)S(1)} collective-permute-done((f32[5,32,256]{2,1,0:T(8,128)S(1)}, f32[5,32,256]{2,1,0:T(8,128)S(1)}, u32[]{:S(2)}, u32[]{:S(2)}) %collective-permute-start.27) | collective-permute-done | bytes 163872 | tf_op jit(solution)/shard_map/ppermute | solution.py:26
  145.6 9.0 %collective-permute-done.26 = f32[5,32,256]{2,1,0:T(8,128)S(1)} collective-permute-done((f32[5,32,256]{2,1,0:T(8,128)S(1)}, f32[5,32,256]{2,1,0:T(8,128)S(1)}, u32[]{:S(2)}, u32[]{:S(2)}) %collective-permute-start.26) | collective-permute-done | bytes 163872 | tf_op jit(solution)/shard_map/ppermute | solution.py:26
  154.7 2.4 %collective-permute-start.29 = (f32[4,32,256]{2,1,0:T(8,128)S(1)}, f32[4,32,256]{2,1,0:T(8,128)S(1)}, u32[]{:S(2)}, u32[]{:S(2)}) collective-permute-start(f32[4,32,256]{2,1,0:T(8,128)S(1)} %slice_divide_fusion), channel_id=1, source_target_pairs={{0,16},{4,20},{8,24},{12,28},{16,0},{20,4},{24,8},{28,12},{1,17},{... | collective-permute-start | bytes 393224 | tf_op jit(solution)/shard_map/ppermute | solution.py:31
  157.1 1.5 collective-permute-start.30
  158.7 1.4 collective-permute-done.29
  160.1 2.0 %collective-permute-done.28 = f32[4,32,256]{2,1,0:T(8,128)S(1)} collective-permute-done((f32[4,32,256]{2,1,0:T(8,128)S(1)}, f32[4,32,256]{2,1,0:T(8,128)S(1)}, u32[]{:S(2)}, u32[]{:S(2)}) %collective-permute-start.28) | collective-permute-done | bytes 131104 | tf_op jit(solution)/shard_map/ppermute | solution.py:31
  162.1 0.9 collective-permute-done.30
  163.2 7.2 %collective-permute-done.18 = bf16[2,256,256]{2,1,0:T(8,128)(2,1)S(1)} collective-permute-done((bf16[2,256,256]{2,1,0:T(8,128)(2,1)S(1)}, bf16[2,256,256]{2,1,0:T(8,128)(2,1)S(1)}, u32[]{:S(2)}, u32[]{:S(2)}) %collective-permute-start.18) | collective-permute-done | bytes 262176 | tf_op jit(solution)/shard_map/ppermute | solution.py:26
  170.3 1.0 fusion.7
  171.3 0.8 copy-done.8
  172.1 2.3 %join.1 = f32[2,2,256,256]{3,2,1,0:T(8,128)} custom-call(s32[19]{0:T(128)} %pad_add_fusion.refs_0_.meta, f32[4,4,32,256]{3,2,1,0:T(8,128)} %copy-done.3, f32[4,4,32,256]{3,2,1,0:T(8,128)} %copy-done.8), custom_call_target="tpu_custom_call" | custom-call | tf_op jit(solution)/shard_map/join/pallas_call | solution.py:331
  (71 shorter events, 4.1 us)
Async XLA Ops:
  0.6 26.9 %copy-start.2 = (f32[2,256,256]{2,1,0:T(8,128)S(1)}, f32[2,256,256]{2,1,0:T(8,128)}, u32[]{:S(2)}) copy-start(f32[2,256,256]{2,1,0:T(8,128)} %param.7) | copy-start | bytes 1572868
  1.6 9.0 %collective-permute-start.9 = (f32[2,2,32,256]{3,2,1,0:T(8,128)S(1)}, f32[2,2,32,256]{3,2,1,0:T(8,128)S(1)}, u32[]{:S(2)}, u32[]{:S(2)}) collective-permute-start(f32[2,2,32,256]{3,2,1,0:T(8,128)S(1)} %constant_dynamic-slice_fusion), channel_id=1, source_target_pairs={{0,3},{1,0},{2,1},{3,2},{4,7},{5,4},{6,5},{7,6},{8,11},{9,8},{10,9... | collective-permute-start | bytes 393224 | tf_op jit(solution)/shard_map/ppermute | solution.py:26
  6.8 11.2 %collective-permute-start.8 = (f32[2,2,32,256]{3,2,1,0:T(8,128)S(1)}, f32[2,2,32,256]{3,2,1,0:T(8,128)S(1)}, u32[]{:S(2)}, u32[]{:S(2)}) collective-permute-start(f32[2,2,32,256]{3,2,1,0:T(8,128)S(1)} %constant_dynamic-slice_fusion), channel_id=1, source_target_pairs={{0,2},{1,3},{2,0},{3,1},{4,6},{5,7},{6,4},{7,5},{8,10},{9,11},{10,... | collective-permute-start | bytes 393224 | tf_op jit(solution)/shard_map/ppermute | solution.py:26
  6.8 11.2 %collective-permute-start.7 = (f32[2,2,32,256]{3,2,1,0:T(8,128)S(1)}, f32[2,2,32,256]{3,2,1,0:T(8,128)S(1)}, u32[]{:S(2)}, u32[]{:S(2)}) collective-permute-start(f32[2,2,32,256]{3,2,1,0:T(8,128)S(1)} %constant_dynamic-slice_fusion), channel_id=1, source_target_pairs={{0,1},{1,2},{2,3},{3,0},{4,5},{5,6},{6,7},{7,4},{8,9},{9,10},{10,1... | collective-permute-start | bytes 393224 | tf_op jit(solution)/shard_map/ppermute | solution.py:26
  18.1 6.3 %collective-permute-start.10 = (f32[1,3,1,2,32,256]{5,4,3,2,1,0:T(8,128)S(1)}, f32[1,3,1,2,32,256]{5,4,3,2,1,0:T(8,128)S(1)}, u32[]{:S(2)}, u32[]{:S(2)}) collective-permute-start(f32[1,3,1,2,32,256]{5,4,3,2,1,0:T(8,128)S(1)} %get-tuple-element.26), channel_id=1, source_target_pairs={{0,8},{4,12},{8,0},{12,4},{16,24},{20,28},{24,16},{28,20},{1,9},{5... | collective-permute-start | bytes 589832 | tf_op jit(solution)/shard_map/ppermute | solution.py:31
  19.6 6.3 %collective-permute-start.13 = (f32[1,3,1,2,32,256]{5,4,3,2,1,0:T(8,128)S(1)}, f32[1,3,1,2,32,256]{5,4,3,2,1,0:T(8,128)S(1)}, u32[]{:S(2)}, u32[]{:S(2)}) collective-permute-start(f32[1,3,1,2,32,256]{5,4,3,2,1,0:T(8,128)S(1)} %get-tuple-element.25), channel_id=1, source_target_pairs={{0,16},{4,20},{8,24},{12,28},{16,0},{20,4},{24,8},{28,12},{1,17},{... | collective-permute-start | bytes 589832 | tf_op jit(solution)/shard_map/ppermute | solution.py:31
  24.4 9.6 %collective-permute-start.11 = (f32[2,3,1,2,32,256]{5,4,3,2,1,0:T(8,128)S(1)}, f32[2,3,1,2,32,256]{5,4,3,2,1,0:T(8,128)S(1)}, u32[]{:S(2)}, u32[]{:S(2)}) collective-permute-start(f32[2,3,1,2,32,256]{5,4,3,2,1,0:T(8,128)S(1)} %pad_maximum_fusion.3), channel_id=1, source_target_pairs={{0,16},{4,20},{8,24},{12,28},{16,0},{20,4},{24,8},{28,12},{1,17},{... | collective-permute-start | bytes 1179656 | tf_op jit(solution)/shard_map/ppermute | solution.py:31
  26.0 39.1 %copy-start.10 = (s32[8,2]{0,1:T(2,128)S(1)}, s32[8,2]{0,1:T(2,128)}, u32[]{:S(2)}) copy-start(s32[8,2]{0,1:T(2,128)} %param.10) | copy-start | bytes 196
  26.0 9.4 %collective-permute-start.14 = (f32[2,3,1,2,32,256]{5,4,3,2,1,0:T(8,128)S(1)}, f32[2,3,1,2,32,256]{5,4,3,2,1,0:T(8,128)S(1)}, u32[]{:S(2)}, u32[]{:S(2)}) collective-permute-start(f32[2,3,1,2,32,256]{5,4,3,2,1,0:T(8,128)S(1)} %pad_maximum_fusion.4), channel_id=1, source_target_pairs={{0,8},{4,12},{8,0},{12,4},{16,24},{20,28},{24,16},{28,20},{1,9},{5... | collective-permute-start | bytes 1179656 | tf_op jit(solution)/shard_map/ppermute | solution.py:31
  27.6 39.9 %copy-start.5 = (bf16[2,256,256]{2,1,0:T(8,128)(2,1)}, bf16[2,256,256]{2,1,0:T(8,128)(2,1)S(1)}, u32[]{:S(2)}) copy-start(bf16[2,256,256]{2,1,0:T(8,128)(2,1)S(1)} %convert_element_type.54.refs_1_) | copy-start | bytes 786436
  27.6 10.4 %collective-permute-start.3 = (bf16[2,256,256]{2,1,0:T(8,128)(2,1)S(1)}, bf16[2,256,256]{2,1,0:T(8,128)(2,1)S(1)}, u32[]{:S(2)}, u32[]{:S(2)}) collective-permute-start(bf16[2,256,256]{2,1,0:T(8,128)(2,1)S(1)} %convert_element_type.54.refs_1_), channel_id=1, source_target_pairs={{4,0},{8,4},{12,8},{16,12},{20,16},{24,20},{28,24},{5,1},{9,5},{13... | collective-permute-start | bytes 786440 | tf_op jit(solution)/shard_map/ppermute | solution.py:21
  34.1 33.5 %copy-start = (f32[4,3,1,2,32,256]{5,4,3,2,1,0:T(8,128)}, f32[4,3,1,2,32,256]{5,4,3,2,1,0:T(8,128)S(1)}, u32[]{:S(2)}) copy-start(f32[4,3,1,2,32,256]{5,4,3,2,1,0:T(8,128)S(1)} %pad_maximum_fusion.refs_10_) | copy-start | bytes 2359300
  34.1 33.4 %collective-permute-start.12 = (f32[4,3,1,2,32,256]{5,4,3,2,1,0:T(8,128)S(1)}, f32[4,3,1,2,32,256]{5,4,3,2,1,0:T(8,128)S(1)}, u32[]{:S(2)}, u32[]{:S(2)}) collective-permute-start(f32[4,3,1,2,32,256]{5,4,3,2,1,0:T(8,128)S(1)} %pad_maximum_fusion.refs_10_), channel_id=1, source_target_pairs={{0,4},{4,0},{8,12},{12,8},{16,20},{20,16},{24,28},{28,24},{1,5},{5... | collective-permute-start | bytes 2359304 | tf_op jit(solution)/shard_map/ppermute | solution.py:31
  35.4 32.1 %copy-start.1 = (f32[4,3,1,2,32,256]{5,4,3,2,1,0:T(8,128)}, f32[4,3,1,2,32,256]{5,4,3,2,1,0:T(8,128)S(1)}, u32[]{:S(2)}) copy-start(f32[4,3,1,2,32,256]{5,4,3,2,1,0:T(8,128)S(1)} %pad_maximum_fusion.1.refs_12_) | copy-start | bytes 2359300
  35.4 32.1 %collective-permute-start.15 = (f32[4,3,1,2,32,256]{5,4,3,2,1,0:T(8,128)S(1)}, f32[4,3,1,2,32,256]{5,4,3,2,1,0:T(8,128)}, u32[]{:S(2)}, u32[]{:S(2)}) collective-permute-start(f32[4,3,1,2,32,256]{5,4,3,2,1,0:T(8,128)S(1)} %pad_maximum_fusion.1.refs_12_), channel_id=1, source_target_pairs={{0,4},{4,0},{8,12},{12,8},{16,20},{20,16},{24,28},{28,24},{1,5},{5... | collective-permute-start | bytes 2359304 | tf_op jit(solution)/shard_map/ppermute | solution.py:31
  35.5 8.8 %collective-permute-start.2 = (bf16[2,256,256]{2,1,0:T(8,128)(2,1)S(1)}, bf16[2,256,256]{2,1,0:T(8,128)(2,1)}, u32[]{:S(2)}, u32[]{:S(2)}) collective-permute-start(bf16[2,256,256]{2,1,0:T(8,128)(2,1)S(1)} %convert_element_type.54.refs_1_), channel_id=1, source_target_pairs={{0,3},{1,0},{2,1},{3,2},{4,7},{5,4},{6,5},{7,6},{8,11},{9,8},{10,9... | collective-permute-start | bytes 786440 | tf_op jit(solution)/shard_map/ppermute | solution.py:26
  36.4 25.4 %collective-permute-start.1 = (bf16[2,256,256]{2,1,0:T(8,128)(2,1)S(1)}, bf16[2,256,256]{2,1,0:T(8,128)(2,1)}, u32[]{:S(2)}, u32[]{:S(2)}) collective-permute-start(bf16[2,256,256]{2,1,0:T(8,128)(2,1)S(1)} %convert_element_type.54.refs_1_), channel_id=1, source_target_pairs={{0,2},{1,3},{2,0},{3,1},{4,6},{5,7},{6,4},{7,5},{8,10},{9,11},{10,... | collective-permute-start | bytes 786440 | tf_op jit(solution)/shard_map/ppermute | solution.py:26
  38.0 29.5 %copy-start.9 = (bf16[2,256,256]{2,1,0:T(8,128)(2,1)}, bf16[2,256,256]{2,1,0:T(8,128)(2,1)S(1)}, u32[]{:S(2)}) copy-start(bf16[2,256,256]{2,1,0:T(8,128)(2,1)S(1)} %collective-permute-done.3.refs_5_) | copy-start | bytes 786436
  38.0 25.1 %collective-permute-start = (bf16[2,256,256]{2,1,0:T(8,128)(2,1)S(1)}, bf16[2,256,256]{2,1,0:T(8,128)(2,1)}, u32[]{:S(2)}, u32[]{:S(2)}) collective-permute-start(bf16[2,256,256]{2,1,0:T(8,128)(2,1)S(1)} %convert_element_type.54.refs_1_), channel_id=1, source_target_pairs={{0,1},{1,2},{2,3},{3,0},{4,5},{5,6},{6,7},{7,4},{8,9},{9,10},{10,1... | collective-permute-start | bytes 786440 | tf_op jit(solution)/shard_map/ppermute | solution.py:26
  44.3 21.6 %collective-permute-start.6 = (bf16[2,256,256]{2,1,0:T(8,128)(2,1)}, bf16[2,256,256]{2,1,0:T(8,128)(2,1)}, u32[]{:S(2)}, u32[]{:S(2)}) collective-permute-start(bf16[2,256,256]{2,1,0:T(8,128)(2,1)} %collective-permute-done.2.refs_4_), channel_id=1, source_target_pairs={{4,0},{8,4},{12,8},{16,12},{20,16},{24,20},{28,24},{5,1},{9,5},{13... | collective-permute-start | bytes 786440 | tf_op jit(solution)/shard_map/ppermute | solution.py:21
  61.8 4.1 %collective-permute-start.5 = (bf16[2,256,256]{2,1,0:T(8,128)(2,1)}, bf16[2,256,256]{2,1,0:T(8,128)(2,1)}, u32[]{:S(2)}, u32[]{:S(2)}) collective-permute-start(bf16[2,256,256]{2,1,0:T(8,128)(2,1)} %collective-permute-done.1.refs_3_), channel_id=1, source_target_pairs={{4,0},{8,4},{12,8},{16,12},{20,16},{24,20},{28,24},{5,1},{9,5},{13... | collective-permute-start | bytes 786440 | tf_op jit(solution)/shard_map/ppermute | solution.py:21
  63.1 4.4 %collective-permute-start.4 = (bf16[2,256,256]{2,1,0:T(8,128)(2,1)}, bf16[2,256,256]{2,1,0:T(8,128)(2,1)}, u32[]{:S(2)}, u32[]{:S(2)}) collective-permute-start(bf16[2,256,256]{2,1,0:T(8,128)(2,1)} %collective-permute-done.refs_2_), channel_id=1, source_target_pairs={{4,0},{8,4},{12,8},{16,12},{20,16},{24,20},{28,24},{5,1},{9,5},{13... | collective-permute-start | bytes 786440 | tf_op jit(solution)/shard_map/ppermute | solution.py:21
  67.5 0.9 copy-start.7
  90.7 15.1 %collective-permute-start.21 = (bf16[4,17,32,256]{3,2,1,0:T(8,128)(2,1)}, bf16[4,17,32,256]{3,2,1,0:T(8,128)(2,1)S(1)}, u32[]{:S(2)}, u32[]{:S(2)}) collective-permute-start(bf16[4,17,32,256]{3,2,1,0:T(8,128)(2,1)} %get-tuple-element.11), channel_id=1, source_target_pairs={{0,4},{4,0},{8,12},{12,8},{16,20},{20,16},{24,28},{28,24},{1,5},{5... | collective-permute-start | bytes 3342344 | tf_op jit(solution)/shard_map/ppermute | solution.py:31
  95.6 25.8 %collective-permute-start.16 = (bf16[4,2,256,256]{3,2,1,0:T(8,128)(2,1)}, bf16[4,2,256,256]{3,2,1,0:T(8,128)(2,1)S(1)}, u32[]{:S(2)}, u32[]{:S(2)}) collective-permute-start(bf16[4,2,256,256]{3,2,1,0:T(8,128)(2,1)} %get-tuple-element.8), channel_id=1, source_target_pairs={{0,4},{4,8},{8,12},{12,16},{16,20},{20,24},{24,28},{1,5},{5,9},{9,... | collective-permute-start | bytes 3145736 | tf_op jit(solution)/shard_map/ppermute | solution.py:21
  97.7 5.1 %collective-permute-start.20 = (s32[17]{0:T(128)S(1)}, s32[17]{0:T(128)S(1)}, u32[]{:S(2)}, u32[]{:S(2)}) collective-permute-start(s32[17]{0:T(128)S(1)} %pad_add_fusion.1), channel_id=1, source_target_pairs={{0,4},{4,8},{8,12},{12,16},{16,20},{20,24},{24,28},{1,5},{5,9},{9,... | collective-permute-start | bytes 212 | tf_op jit(solution)/shard_map/ppermute | solution.py:21
  102.8 0.5 copy-start.11
  107.9 13.5 %copy-start.4 = (bf16[4,2,256,256]{3,2,1,0:T(8,128)(2,1)S(1)}, bf16[4,2,256,256]{3,2,1,0:T(8,128)(2,1)}, u32[]{:S(2)}) copy-start(bf16[4,2,256,256]{3,2,1,0:T(8,128)(2,1)} %get-tuple-element.7) | copy-start | bytes 3145732
  108.0 19.4 %collective-permute-start.22 = (bf16[17,32,256]{2,1,0:T(8,128)(2,1)S(1)}, bf16[17,32,256]{2,1,0:T(8,128)(2,1)S(1)}, u32[]{:S(2)}, u32[]{:S(2)}) collective-permute-start(bf16[17,32,256]{2,1,0:T(8,128)(2,1)S(1)} %get-tuple-element.16), channel_id=1, source_target_pairs={{0,8},{4,12},{8,0},{12,4},{16,24},{20,28},{24,16},{28,20},{1,9},{5... | collective-permute-start | bytes 835592 | tf_op jit(solution)/shard_map/ppermute | solution.py:31
  119.9 10.4 %collective-permute-start.24 = (bf16[17,32,256]{2,1,0:T(8,128)(2,1)S(1)}, bf16[17,32,256]{2,1,0:T(8,128)(2,1)S(1)}, u32[]{:S(2)}, u32[]{:S(2)}) collective-permute-start(bf16[17,32,256]{2,1,0:T(8,128)(2,1)S(1)} %get-tuple-element.17), channel_id=1, source_target_pairs={{0,24},{4,28},{8,16},{12,20},{16,8},{20,12},{24,0},{28,4},{1,25},{... | collective-permute-start | bytes 835592 | tf_op jit(solution)/shard_map/ppermute | solution.py:31
  121.2 11.9 %collective-permute-start.23 = (bf16[17,32,256]{2,1,0:T(8,128)(2,1)S(1)}, bf16[17,32,256]{2,1,0:T(8,128)(2,1)S(1)}, u32[]{:S(2)}, u32[]{:S(2)}) collective-permute-start(bf16[17,32,256]{2,1,0:T(8,128)(2,1)S(1)} %get-tuple-element.18), channel_id=1, source_target_pairs={{0,16},{4,20},{8,24},{12,28},{16,0},{20,4},{24,8},{28,12},{1,17},{... | collective-permute-start | bytes 835592 | tf_op jit(solution)/shard_map/ppermute | solution.py:31
  133.3 12.3 %collective-permute-start.27 = (f32[5,32,256]{2,1,0:T(8,128)S(1)}, f32[5,32,256]{2,1,0:T(8,128)S(1)}, u32[]{:S(2)}, u32[]{:S(2)}) collective-permute-start(f32[5,32,256]{2,1,0:T(8,128)S(1)} %concatenate.73), channel_id=1, source_target_pairs={{0,3},{1,0},{2,1},{3,2},{4,7},{5,4},{6,5},{7,6},{8,11},{9,8},{10,9... | collective-permute-start | bytes 491528 | tf_op jit(solution)/shard_map/ppermute | solution.py:26
  133.4 29.7 %copy-start.6 = (f32[256,256]{1,0:T(8,128)S(1)}, f32[256,256]{1,0:T(8,128)}, u32[]{:S(2)}) copy-start(f32[256,256]{1,0:T(8,128)} %illumination.1) | copy-start | bytes 786436
  133.5 12.2 %collective-permute-start.25 = (f32[5,32,256]{2,1,0:T(8,128)S(1)}, f32[5,32,256]{2,1,0:T(8,128)S(1)}, u32[]{:S(2)}, u32[]{:S(2)}) collective-permute-start(f32[5,32,256]{2,1,0:T(8,128)S(1)} %get-tuple-element.27), channel_id=1, source_target_pairs={{0,1},{1,2},{2,3},{3,0},{4,5},{5,6},{6,7},{7,4},{8,9},{9,10},{10,1... | collective-permute-start | bytes 491528 | tf_op jit(solution)/shard_map/ppermute | solution.py:26
  135.5 19.1 %collective-permute-start.26 = (f32[5,32,256]{2,1,0:T(8,128)S(1)}, f32[5,32,256]{2,1,0:T(8,128)S(1)}, u32[]{:S(2)}, u32[]{:S(2)}) collective-permute-start(f32[5,32,256]{2,1,0:T(8,128)S(1)} %get-tuple-element.28), channel_id=1, source_target_pairs={{0,2},{1,3},{2,0},{3,1},{4,6},{5,7},{6,4},{7,5},{8,10},{9,11},{10,... | collective-permute-start | bytes 491528 | tf_op jit(solution)/shard_map/ppermute | solution.py:26
  136.0 27.2 %collective-permute-start.17 = (bf16[2,256,256]{2,1,0:T(8,128)(2,1)S(1)}, bf16[2,256,256]{2,1,0:T(8,128)(2,1)S(1)}, u32[]{:S(2)}, u32[]{:S(2)}) collective-permute-start(bf16[2,256,256]{2,1,0:T(8,128)(2,1)S(1)} %get-tuple-element.19), channel_id=1, source_target_pairs={{0,1},{1,2},{2,3},{3,0},{4,5},{5,6},{6,7},{7,4},{8,9},{9,10},{10,1... | collective-permute-start | bytes 786440 | tf_op jit(solution)/shard_map/ppermute | solution.py:26
  138.0 25.2 %collective-permute-start.19 = (bf16[2,256,256]{2,1,0:T(8,128)(2,1)S(1)}, bf16[2,256,256]{2,1,0:T(8,128)(2,1)S(1)}, u32[]{:S(2)}, u32[]{:S(2)}) collective-permute-start(bf16[2,256,256]{2,1,0:T(8,128)(2,1)S(1)} %get-tuple-element.20), channel_id=1, source_target_pairs={{0,3},{1,0},{2,1},{3,2},{4,7},{5,4},{6,5},{7,6},{8,11},{9,8},{10,9... | collective-permute-start | bytes 786440 | tf_op jit(solution)/shard_map/ppermute | solution.py:26
  154.7 5.3 %collective-permute-start.29 = (f32[4,32,256]{2,1,0:T(8,128)S(1)}, f32[4,32,256]{2,1,0:T(8,128)S(1)}, u32[]{:S(2)}, u32[]{:S(2)}) collective-permute-start(f32[4,32,256]{2,1,0:T(8,128)S(1)} %slice_divide_fusion), channel_id=1, source_target_pairs={{0,16},{4,20},{8,24},{12,28},{16,0},{20,4},{24,8},{28,12},{1,17},{... | collective-permute-start | bytes 393224 | tf_op jit(solution)/shard_map/ppermute | solution.py:31
  157.1 5.0 %collective-permute-start.28 = (f32[4,32,256]{2,1,0:T(8,128)S(1)}, f32[4,32,256]{2,1,0:T(8,128)S(1)}, u32[]{:S(2)}, u32[]{:S(2)}) collective-permute-start(f32[4,32,256]{2,1,0:T(8,128)S(1)} %slice_divide_fusion), channel_id=1, source_target_pairs={{0,8},{4,12},{8,0},{12,4},{16,24},{20,28},{24,16},{28,20},{1,9},{5... | collective-permute-start | bytes 393224 | tf_op jit(solution)/shard_map/ppermute | solution.py:31
  157.1 5.9 %collective-permute-start.30 = (f32[4,32,256]{2,1,0:T(8,128)S(1)}, f32[4,32,256]{2,1,0:T(8,128)S(1)}, u32[]{:S(2)}, u32[]{:S(2)}) collective-permute-start(f32[4,32,256]{2,1,0:T(8,128)S(1)} %slice_divide_fusion), channel_id=1, source_target_pairs={{0,24},{4,28},{8,16},{12,20},{16,8},{20,12},{24,0},{28,4},{1,25},{... | collective-permute-start | bytes 393224 | tf_op jit(solution)/shard_map/ppermute | solution.py:31
  160.1 10.3 %collective-permute-start.18 = (bf16[2,256,256]{2,1,0:T(8,128)(2,1)S(1)}, bf16[2,256,256]{2,1,0:T(8,128)(2,1)S(1)}, u32[]{:S(2)}, u32[]{:S(2)}) collective-permute-start(bf16[2,256,256]{2,1,0:T(8,128)(2,1)S(1)} %get-tuple-element.21), channel_id=1, source_target_pairs={{0,2},{1,3},{2,0},{3,1},{4,6},{5,7},{6,4},{7,5},{8,10},{9,11},{10,... | collective-permute-start | bytes 786440 | tf_op jit(solution)/shard_map/ppermute | solution.py:26
  163.0 8.3 %copy-start.3 = (f32[4,4,32,256]{3,2,1,0:T(8,128)}, f32[4,4,32,256]{3,2,1,0:T(8,128)S(1)}, u32[]{:S(2)}) copy-start(f32[4,4,32,256]{3,2,1,0:T(8,128)S(1)} %pad_maximum_fusion.2.steps) | copy-start | bytes 1572868
  163.0 8.3 %collective-permute-start.31 = (f32[4,4,32,256]{3,2,1,0:T(8,128)S(1)}, f32[4,4,32,256]{3,2,1,0:T(8,128)S(1)}, u32[]{:S(2)}, u32[]{:S(2)}) collective-permute-start(f32[4,4,32,256]{3,2,1,0:T(8,128)S(1)} %pad_maximum_fusion.2.steps), channel_id=1, source_target_pairs={{0,4},{4,0},{8,12},{12,8},{16,20},{20,16},{24,28},{28,24},{1,5},{5... | collective-permute-start | bytes 1572872 | tf_op jit(solution)/shard_map/ppermute | solution.py:31
  171.3 0.8 copy-start.8

commit v2 on v1

--- a/solution.py
+++ b/solution.py
@@ -212,13 +212,14 @@
 
 
 def join_kernel(local, spread, part):
-    def body(meta, steps, mates, out):
+    def body(meta, *refs):
+        out = refs[spread]
         for k in range(spread):
             at = pl.multiple_of(((meta[0] % spread) ^ k) * part, part)
             for m in range(local):
                 for ch in range(2):
-                    pick = mates if k % 2 else steps
-                    out[m, ch, pl.ds(at, part), :] = pick[k // 2, 2 * m + ch]
+                    pick = refs[k // 2 + k % 2 * (spread // 2)]
+                    out[m, ch, pl.ds(at, part), :] = pick[2 * m + ch]
 
     return body
 
@@ -322,19 +323,18 @@
     step = None
     for d in range(tiles):
         share = jnp.concatenate([total[2 * local * d : 2 * local * (d + 1)], total[2 * modes :]])
-        share = rotated(share, "tile", d) if d else share
+        share = rotated(share.astype(bf16), "tile", d).astype(f32) if d else share
         step = share if step is None else step + share
     step = step[: 2 * local] / (step[2 * local] + damping)
     steps = [step] + [swapped(step, "scan", 2 * k) for k in range(1, spread // 2)]
-    steps = jnp.stack(steps)
-    mates = swapped(steps, "scan", 1)
+    steps += [swapped(value, "scan", 1) for value in steps]
     probe_step = pl.pallas_call(
         join_kernel(local, spread, part),
         out_shape=jax.ShapeDtypeStruct(probe_modes.shape, f32),
-        in_specs=[smem, vmem, vmem],
+        in_specs=[smem] + [vmem] * spread,
         out_specs=vmem,
         name="join",
-    )(meta, steps, mates)
+    )(meta, *steps)
     return (new_object, probe_step)
 
 

time: 175 us -> 171 us (0.977)
  waiting for transfers between devices: 80.1 us -> 75.1 us
    ppermute x14 -> x17, waiting for transfers between devices: 25.2 us -> 22.3 us  [swapped(): return lax.ppermute(value, axis, pairs)]
    ppermute x12, waiting for transfers between devices: 52.7 us -> 50.4 us  [rotated(): lax.ppermute(value, axis, [(i, (i + steps) % count) for i in range(count)])]
    ppermute x14 -> x17, starting transfers between devices: 28.8 us -> 27.6 us  [swapped(): return lax.ppermute(value, axis, pairs)]
  transfers between devices with their start and end apart: 32 -> 35, of which waited for: 18 -> 18; matrix products, arithmetic and copies ran while one was open for 3% -> 3% of each run, Pallas kernels for 1% -> 1%
where the time goes in v2:
time: 171 us; the launch traced here: 170 us
  waiting for transfers between devices  75.1 us (44%)
  starting transfers between devices  57.9 us (34%)
  Pallas kernels  27 us (16%)
  other arithmetic  4.57 us (3%)
  local copies, waits for them, and re-layouts  4.07 us (2%)
  between operations  1.74 us (1%)
    ppermute x12, waiting for transfers between devices, rotated(): lax.ppermute(value, axis, [(i, (i + steps) % count) for i in range(count)])  50.4 us
    ppermute x17, starting transfers between devices, swapped(): return lax.ppermute(value, axis, pairs)  27.6 us
    ppermute x17, waiting for transfers between devices, swapped(): return lax.ppermute(value, axis, pairs)  22.3 us
    pallas_call x1, Pallas kernels, update(): pl.pallas_call(main_kernel(tiles, slots, modes, width, band, spread, part...  22.2 us
    ppermute x12, starting transfers between devices, rotated(): lax.ppermute(value, axis, [(i, (i + steps) % count) for i in range(count)])  18.6 us
    ppermute x6, starting transfers between devices, shifted(): return lax.ppermute(value, axis, pairs)  11.6 us
  transfers between devices with their start and end apart: 35, of which 18 were waited for; matrix products, arithmetic and copies ran while one was open for 3% of the time, Pallas kernels for 1%

profile of v2, /device:TPU:0, one launch (start us, length us, event | category | flops | bytes accessed | tf_op | source)
XLA Modules:
  0.0 170.3 jit_solution(2809583546752015280)
XLA Ops:
  0.7 1.0 constant_dynamic-slice_fusion
  1.6 5.1 %collective-permute-start.9 = (f32[2,2,32,256]{3,2,1,0:T(8,128)S(1)}, f32[2,2,32,256]{3,2,1,0:T(8,128)S(1)}, u32[]{:S(2)}, u32[]{:S(2)}) collective-permute-start(f32[2,2,32,256]{3,2,1,0:T(8,128)S(1)} %constant_dynamic-slice_fusion), channel_id=1, source_target_pairs={{0,3},{1,0},{2,1},{3,2},{4,7},{5,4},{6,5},{7,6},{8,11},{9,8},{10,9... | collective-permute-start | bytes 393224 | tf_op jit(solution)/shard_map/ppermute | solution.py:26
  6.8 1.0 collective-permute-start.7
  7.8 2.9 %collective-permute-done.9 = f32[2,2,32,256]{3,2,1,0:T(8,128)S(1)} collective-permute-done((f32[2,2,32,256]{3,2,1,0:T(8,128)S(1)}, f32[2,2,32,256]{3,2,1,0:T(8,128)S(1)}, u32[]{:S(2)}, u32[]{:S(2)}) %collective-permute-start.9) | collective-permute-done | bytes 131104 | tf_op jit(solution)/shard_map/ppermute | solution.py:26
  10.7 7.3 %collective-permute-done.8 = f32[2,2,32,256]{3,2,1,0:T(8,128)S(1)} collective-permute-done((f32[2,2,32,256]{3,2,1,0:T(8,128)S(1)}, f32[2,2,32,256]{3,2,1,0:T(8,128)S(1)}, u32[]{:S(2)}, u32[]{:S(2)}) %collective-permute-start.8) | collective-permute-done | bytes 131104 | tf_op jit(solution)/shard_map/ppermute | solution.py:26
  18.1 1.6 collective-permute-start.10
  19.6 1.5 collective-permute-start.13
  21.1 3.2 %collective-permute-done.10 = f32[1,3,1,2,32,256]{5,4,3,2,1,0:T(8,128)S(1)} collective-permute-done((f32[1,3,1,2,32,256]{5,4,3,2,1,0:T(8,128)S(1)}, f32[1,3,1,2,32,256]{5,4,3,2,1,0:T(8,128)S(1)}, u32[]{:S(2)}, u32[]{:S(2)}) %collective-permute-start.10) | collective-permute-done | bytes 196640 | tf_op jit(solution)/shard_map/ppermute | solution.py:31
  24.4 1.6 collective-permute-start.11
  26.0 1.6 collective-permute-start.14
  27.6 1.3 collective-permute-start.3
  28.9 5.1 %collective-permute-done.11 = f32[2,3,1,2,32,256]{5,4,3,2,1,0:T(8,128)S(1)} collective-permute-done((f32[2,3,1,2,32,256]{5,4,3,2,1,0:T(8,128)S(1)}, f32[2,3,1,2,32,256]{5,4,3,2,1,0:T(8,128)S(1)}, u32[]{:S(2)}, u32[]{:S(2)}) %collective-permute-start.11) | collective-permute-done | bytes 393248 | tf_op jit(solution)/shard_map/ppermute | solution.py:31
  34.2 1.2 collective-permute-done.14
  35.5 0.9 collective-permute-start.2
  36.4 1.6 collective-permute-start.1
  38.0 1.9 %collective-permute-start = (bf16[2,256,256]{2,1,0:T(8,128)(2,1)S(1)}, bf16[2,256,256]{2,1,0:T(8,128)(2,1)}, u32[]{:S(2)}, u32[]{:S(2)}) collective-permute-start(bf16[2,256,256]{2,1,0:T(8,128)(2,1)S(1)} %convert_element_type.66.refs_1_), channel_id=1, source_target_pairs={{0,1},{1,2},{2,3},{3,0},{4,5},{5,6},{6,7},{7,4},{8,9},{9,10},{10,1... | collective-permute-start | bytes 786440 | tf_op jit(solution)/shard_map/ppermute | solution.py:26
  40.0 4.3 %collective-permute-done.2.refs_4_ = bf16[2,256,256]{2,1,0:T(8,128)(2,1)} collective-permute-done((bf16[2,256,256]{2,1,0:T(8,128)(2,1)S(1)}, bf16[2,256,256]{2,1,0:T(8,128)(2,1)}, u32[]{:S(2)}, u32[]{:S(2)}) %collective-permute-start.2) | collective-permute-done | bytes 262176 | tf_op jit(solution)/shard_map/ppermute | solution.py:26
  44.3 1.3 collective-permute-start.6
  45.6 16.2 %collective-permute-done.1.refs_3_ = bf16[2,256,256]{2,1,0:T(8,128)(2,1)} collective-permute-done((bf16[2,256,256]{2,1,0:T(8,128)(2,1)S(1)}, bf16[2,256,256]{2,1,0:T(8,128)(2,1)}, u32[]{:S(2)}, u32[]{:S(2)}) %collective-permute-start.1) | collective-permute-done | bytes 262176 | tf_op jit(solution)/shard_map/ppermute | solution.py:26
  61.8 1.3 collective-permute-start.5
  63.1 1.3 collective-permute-start.4
  65.2 0.6 pad_add_fusion.refs_0_.meta
  65.8 1.7 %collective-permute-done.4.refs_6_ = bf16[2,256,256]{2,1,0:T(8,128)(2,1)} collective-permute-done((bf16[2,256,256]{2,1,0:T(8,128)(2,1)}, bf16[2,256,256]{2,1,0:T(8,128)(2,1)}, u32[]{:S(2)}, u32[]{:S(2)}) %collective-permute-start.4) | collective-permute-done | bytes 262176 | tf_op jit(solution)/shard_map/ppermute | solution.py:21
  67.6 0.9 copy-done.6
  68.4 22.2 %update.1 = (bf16[4,2,256,256]{3,2,1,0:T(8,128)(2,1)}, bf16[4,2,256,256]{3,2,1,0:T(8,128)(2,1)}, f32[256,256]{1,0:T(8,128)}, bf16[4,17,32,256]{3,2,1,0:T(8,128)(2,1)}, f32[4,17,32,256]{3,2,1,0:T(8,128)}) custom-call(s32[19]{0:T(128)} %pad_add_fusion.refs_0_.meta, bf16[2,256,256]{2,1,0:T(8,128)(2,1)} %copy-done.4, ...), custom_call_target="tpu_custom_call" | custom-call | tf_op jit(solution)/shard_map/update/pallas_call | solution.py:262
  90.7 5.0 %collective-permute-start.21 = (bf16[4,17,32,256]{3,2,1,0:T(8,128)(2,1)}, bf16[4,17,32,256]{3,2,1,0:T(8,128)(2,1)S(1)}, u32[]{:S(2)}, u32[]{:S(2)}) collective-permute-start(bf16[4,17,32,256]{3,2,1,0:T(8,128)(2,1)} %get-tuple-element.11), channel_id=1, source_target_pairs={{0,4},{4,0},{8,12},{12,8},{16,20},{20,16},{24,28},{28,24},{1,5},{5... | collective-permute-start | bytes 3342344 | tf_op jit(solution)/shard_map/ppermute | solution.py:31
  95.7 2.0 %collective-permute-start.16 = (bf16[4,2,256,256]{3,2,1,0:T(8,128)(2,1)}, bf16[4,2,256,256]{3,2,1,0:T(8,128)(2,1)S(1)}, u32[]{:S(2)}, u32[]{:S(2)}) collective-permute-start(bf16[4,2,256,256]{3,2,1,0:T(8,128)(2,1)} %get-tuple-element.8), channel_id=1, source_target_pairs={{0,4},{4,8},{8,12},{12,16},{16,20},{20,24},{24,28},{1,5},{5,9},{9,... | collective-permute-start | bytes 3145736 | tf_op jit(solution)/shard_map/ppermute | solution.py:21
  97.7 4.5 %collective-permute-start.20 = (s32[17]{0:T(128)S(1)}, s32[17]{0:T(128)S(1)}, u32[]{:S(2)}, u32[]{:S(2)}) collective-permute-start(s32[17]{0:T(128)S(1)} %pad_add_fusion.1), channel_id=1, source_target_pairs={{0,4},{4,8},{8,12},{12,16},{16,20},{20,24},{24,28},{1,5},{5,9},{9,... | collective-permute-start | bytes 212 | tf_op jit(solution)/shard_map/ppermute | solution.py:21
  102.2 0.6 collective-permute-done.20.above
  103.4 2.4 %illumination.1 = f32[256,256]{1,0:T(8,128)} custom-call(s32[19]{0:T(128)} %pad_add_fusion.refs_0_.meta, s32[17]{0:T(128)} %copy-done.17, f32[256,256]{1,0:T(8,128)} %get-tuple-element.9.power), custom_call_target="tpu_custom_call" | custom-call | tf_op jit(solution)/shard_map/illumination/pallas_call | solution.py:305
  105.8 2.1 %fusion.14 = (bf16[4,17,32,256]{3,2,1,0:T(8,128)(2,1)S(1)}, f32[4,17,32,256]{3,2,1,0:T(8,128)S(1)}) fusion(f32[4,17,32,256]{3,2,1,0:T(8,128)} %get-tuple-element.10, bf16[4,17,32,256]{3,2,1,0:T(8,128)(2,1)S(1)} %collective-permute-done.21), kind=kLoop, calls=%fused_computation.38 | loop fusion | flops 1671168 | bytes 6684672 | tf_op jit(solution)/shard_map/convert.9
  108.0 11.9 %collective-permute-start.22 = (bf16[17,32,256]{2,1,0:T(8,128)(2,1)S(1)}, bf16[17,32,256]{2,1,0:T(8,128)(2,1)S(1)}, u32[]{:S(2)}, u32[]{:S(2)}) collective-permute-start(bf16[17,32,256]{2,1,0:T(8,128)(2,1)S(1)} %get-tuple-element.18), channel_id=1, source_target_pairs={{0,8},{4,12},{8,0},{12,4},{16,24},{20,28},{24,16},{28,20},{1,9},{5... | collective-permute-start | bytes 835592 | tf_op jit(solution)/shard_map/ppermute | solution.py:31
  119.9 1.3 collective-permute-start.24
  121.7 5.6 %collective-permute-done.22 = bf16[17,32,256]{2,1,0:T(8,128)(2,1)S(1)} collective-permute-done((bf16[17,32,256]{2,1,0:T(8,128)(2,1)S(1)}, bf16[17,32,256]{2,1,0:T(8,128)(2,1)S(1)}, u32[]{:S(2)}, u32[]{:S(2)}) %collective-permute-start.22) | collective-permute-done | bytes 278560 | tf_op jit(solution)/shard_map/ppermute | solution.py:31
  127.4 2.8 %collective-permute-done.24 = bf16[17,32,256]{2,1,0:T(8,128)(2,1)S(1)} collective-permute-done((bf16[17,32,256]{2,1,0:T(8,128)(2,1)S(1)}, bf16[17,32,256]{2,1,0:T(8,128)(2,1)S(1)}, u32[]{:S(2)}, u32[]{:S(2)}) %collective-permute-start.24) | collective-permute-done | bytes 278560 | tf_op jit(solution)/shard_map/ppermute | solution.py:31
  130.2 2.9 %collective-permute-done.23 = bf16[17,32,256]{2,1,0:T(8,128)(2,1)S(1)} collective-permute-done((bf16[17,32,256]{2,1,0:T(8,128)(2,1)S(1)}, bf16[17,32,256]{2,1,0:T(8,128)(2,1)S(1)}, u32[]{:S(2)}, u32[]{:S(2)}) %collective-permute-start.23) | collective-permute-done | bytes 278560 | tf_op jit(solution)/shard_map/ppermute | solution.py:31
  133.9 3.3 %collective-permute-start.27 = (bf16[5,32,256]{2,1,0:T(8,128)(2,1)S(1)}, bf16[5,32,256]{2,1,0:T(8,128)(2,1)S(1)}, u32[]{:S(2)}, u32[]{:S(2)}) collective-permute-start(bf16[5,32,256]{2,1,0:T(8,128)(2,1)S(1)} %concatenate.75), channel_id=1, source_target_pairs={{0,3},{1,0},{2,1},{3,2},{4,7},{5,4},{6,5},{7,6},{8,11},{9,8},{10,9... | collective-permute-start | bytes 245768 | tf_op jit(solution)/shard_map/ppermute | solution.py:26
  137.3 0.6 collective-permute-start.17
  137.9 3.3 %collective-permute-start.19 = (bf16[2,256,256]{2,1,0:T(8,128)(2,1)S(1)}, bf16[2,256,256]{2,1,0:T(8,128)(2,1)S(1)}, u32[]{:S(2)}, u32[]{:S(2)}) collective-permute-start(bf16[2,256,256]{2,1,0:T(8,128)(2,1)S(1)} %get-tuple-element.22), channel_id=1, source_target_pairs={{0,3},{1,0},{2,1},{3,2},{4,7},{5,4},{6,5},{7,6},{8,11},{9,8},{10,9... | collective-permute-start | bytes 786440 | tf_op jit(solution)/shard_map/ppermute | solution.py:26
  141.5 4.5 %collective-permute-done.26 = bf16[5,32,256]{2,1,0:T(8,128)(2,1)S(1)} collective-permute-done((bf16[5,32,256]{2,1,0:T(8,128)(2,1)S(1)}, bf16[5,32,256]{2,1,0:T(8,128)(2,1)S(1)}, u32[]{:S(2)}, u32[]{:S(2)}) %collective-permute-start.26) | collective-permute-done | bytes 81952 | tf_op jit(solution)/shard_map/ppermute | solution.py:26
  146.5 1.8 %collective-permute-start.29 = (f32[4,32,256]{2,1,0:T(8,128)S(1)}, f32[4,32,256]{2,1,0:T(8,128)S(1)}, u32[]{:S(2)}, u32[]{:S(2)}) collective-permute-start(f32[4,32,256]{2,1,0:T(8,128)S(1)} %slice_divide_fusion.refs_0_), channel_id=1, source_target_pairs={{0,16},{4,20},{8,24},{12,28},{16,0},{20,4},{24,8},{28,12},{1,17},{... | collective-permute-start | bytes 393224 | tf_op jit(solution)/shard_map/ppermute | solution.py:31
  148.4 1.3 collective-permute-done.17
  150.0 2.6 %collective-permute-done.19 = bf16[2,256,256]{2,1,0:T(8,128)(2,1)S(1)} collective-permute-done((bf16[2,256,256]{2,1,0:T(8,128)(2,1)S(1)}, bf16[2,256,256]{2,1,0:T(8,128)(2,1)S(1)}, u32[]{:S(2)}, u32[]{:S(2)}) %collective-permute-start.19) | collective-permute-done | bytes 262176 | tf_op jit(solution)/shard_map/ppermute | solution.py:26
  153.2 1.4 collective-permute-done.28.refs_1_
  154.6 10.9 %collective-permute-done.18 = bf16[2,256,256]{2,1,0:T(8,128)(2,1)S(1)} collective-permute-done((bf16[2,256,256]{2,1,0:T(8,128)(2,1)S(1)}, bf16[2,256,256]{2,1,0:T(8,128)(2,1)S(1)}, u32[]{:S(2)}, u32[]{:S(2)}) %collective-permute-start.18) | collective-permute-done | bytes 262176 | tf_op jit(solution)/shard_map/ppermute | solution.py:26
  165.6 1.0 fusion.7
  167.3 0.6 copy-done.15
  168.0 2.3 %join.1 = f32[2,2,256,256]{3,2,1,0:T(8,128)} custom-call(s32[19]{0:T(128)} %pad_add_fusion.refs_0_.meta, f32[4,32,256]{2,1,0:T(8,128)} %copy-done.7, f32[4,32,256]{2,1,0:T(8,128)} %copy-done.11, f32[4,32,256]{2,1,0:T(8,128)} %copy-done.10, f32[4,32,256]{2,1,0:T(8,128)} %copy-done.9, f32[4,32,256]{2,1,0:T(8,128)} %copy-done.12, f32[4,32,256]{2,1,0:T(8,128)} %copy-done.15, ...), custom_call_target="tpu_custom_call" | custom-call | tf_op jit(solution)/shard_map/join/pallas_call | solution.py:331
  (89 shorter events, 5.1 us)
Async XLA Ops:
  0.6 26.9 %copy-start.2 = (f32[2,256,256]{2,1,0:T(8,128)S(1)}, f32[2,256,256]{2,1,0:T(8,128)}, u32[]{:S(2)}) copy-start(f32[2,256,256]{2,1,0:T(8,128)} %param.7) | copy-start | bytes 1572868
  1.6 9.0 %collective-permute-start.9 = (f32[2,2,32,256]{3,2,1,0:T(8,128)S(1)}, f32[2,2,32,256]{3,2,1,0:T(8,128)S(1)}, u32[]{:S(2)}, u32[]{:S(2)}) collective-permute-start(f32[2,2,32,256]{3,2,1,0:T(8,128)S(1)} %constant_dynamic-slice_fusion), channel_id=1, source_target_pairs={{0,3},{1,0},{2,1},{3,2},{4,7},{5,4},{6,5},{7,6},{8,11},{9,8},{10,9... | collective-permute-start | bytes 393224 | tf_op jit(solution)/shard_map/ppermute | solution.py:26
  6.8 11.2 %collective-permute-start.8 = (f32[2,2,32,256]{3,2,1,0:T(8,128)S(1)}, f32[2,2,32,256]{3,2,1,0:T(8,128)S(1)}, u32[]{:S(2)}, u32[]{:S(2)}) collective-permute-start(f32[2,2,32,256]{3,2,1,0:T(8,128)S(1)} %constant_dynamic-slice_fusion), channel_id=1, source_target_pairs={{0,2},{1,3},{2,0},{3,1},{4,6},{5,7},{6,4},{7,5},{8,10},{9,11},{10,... | collective-permute-start | bytes 393224 | tf_op jit(solution)/shard_map/ppermute | solution.py:26
  6.8 11.2 %collective-permute-start.7 = (f32[2,2,32,256]{3,2,1,0:T(8,128)S(1)}, f32[2,2,32,256]{3,2,1,0:T(8,128)S(1)}, u32[]{:S(2)}, u32[]{:S(2)}) collective-permute-start(f32[2,2,32,256]{3,2,1,0:T(8,128)S(1)} %constant_dynamic-slice_fusion), channel_id=1, source_target_pairs={{0,1},{1,2},{2,3},{3,0},{4,5},{5,6},{6,7},{7,4},{8,9},{9,10},{10,1... | collective-permute-start | bytes 393224 | tf_op jit(solution)/shard_map/ppermute | solution.py:26
  18.1 6.3 %collective-permute-start.10 = (f32[1,3,1,2,32,256]{5,4,3,2,1,0:T(8,128)S(1)}, f32[1,3,1,2,32,256]{5,4,3,2,1,0:T(8,128)S(1)}, u32[]{:S(2)}, u32[]{:S(2)}) collective-permute-start(f32[1,3,1,2,32,256]{5,4,3,2,1,0:T(8,128)S(1)} %get-tuple-element.25), channel_id=1, source_target_pairs={{0,8},{4,12},{8,0},{12,4},{16,24},{20,28},{24,16},{28,20},{1,9},{5... | collective-permute-start | bytes 589832 | tf_op jit(solution)/shard_map/ppermute | solution.py:31
  19.6 6.3 %collective-permute-start.13 = (f32[1,3,1,2,32,256]{5,4,3,2,1,0:T(8,128)S(1)}, f32[1,3,1,2,32,256]{5,4,3,2,1,0:T(8,128)S(1)}, u32[]{:S(2)}, u32[]{:S(2)}) collective-permute-start(f32[1,3,1,2,32,256]{5,4,3,2,1,0:T(8,128)S(1)} %get-tuple-element.24), channel_id=1, source_target_pairs={{0,16},{4,20},{8,24},{12,28},{16,0},{20,4},{24,8},{28,12},{1,17},{... | collective-permute-start | bytes 589832 | tf_op jit(solution)/shard_map/ppermute | solution.py:31
  24.4 9.6 %collective-permute-start.11 = (f32[2,3,1,2,32,256]{5,4,3,2,1,0:T(8,128)S(1)}, f32[2,3,1,2,32,256]{5,4,3,2,1,0:T(8,128)S(1)}, u32[]{:S(2)}, u32[]{:S(2)}) collective-permute-start(f32[2,3,1,2,32,256]{5,4,3,2,1,0:T(8,128)S(1)} %pad_maximum_fusion.2), channel_id=1, source_target_pairs={{0,16},{4,20},{8,24},{12,28},{16,0},{20,4},{24,8},{28,12},{1,17},{... | collective-permute-start | bytes 1179656 | tf_op jit(solution)/shard_map/ppermute | solution.py:31
  26.0 39.1 %copy-start.16 = (s32[8,2]{0,1:T(2,128)S(1)}, s32[8,2]{0,1:T(2,128)}, u32[]{:S(2)}) copy-start(s32[8,2]{0,1:T(2,128)} %param.10) | copy-start | bytes 196
  26.0 9.4 %collective-permute-start.14 = (f32[2,3,1,2,32,256]{5,4,3,2,1,0:T(8,128)S(1)}, f32[2,3,1,2,32,256]{5,4,3,2,1,0:T(8,128)S(1)}, u32[]{:S(2)}, u32[]{:S(2)}) collective-permute-start(f32[2,3,1,2,32,256]{5,4,3,2,1,0:T(8,128)S(1)} %pad_maximum_fusion.3), channel_id=1, source_target_pairs={{0,8},{4,12},{8,0},{12,4},{16,24},{20,28},{24,16},{28,20},{1,9},{5... | collective-permute-start | bytes 1179656 | tf_op jit(solution)/shard_map/ppermute | solution.py:31
  27.6 39.9 %copy-start.4 = (bf16[2,256,256]{2,1,0:T(8,128)(2,1)}, bf16[2,256,256]{2,1,0:T(8,128)(2,1)S(1)}, u32[]{:S(2)}) copy-start(bf16[2,256,256]{2,1,0:T(8,128)(2,1)S(1)} %convert_element_type.66.refs_1_) | copy-start | bytes 786436
  27.6 10.4 %collective-permute-start.3 = (bf16[2,256,256]{2,1,0:T(8,128)(2,1)S(1)}, bf16[2,256,256]{2,1,0:T(8,128)(2,1)S(1)}, u32[]{:S(2)}, u32[]{:S(2)}) collective-permute-start(bf16[2,256,256]{2,1,0:T(8,128)(2,1)S(1)} %convert_element_type.66.refs_1_), channel_id=1, source_target_pairs={{4,0},{8,4},{12,8},{16,12},{20,16},{24,20},{28,24},{5,1},{9,5},{13... | collective-permute-start | bytes 786440 | tf_op jit(solution)/shard_map/ppermute | solution.py:21
  34.1 33.5 %copy-start = (f32[4,3,1,2,32,256]{5,4,3,2,1,0:T(8,128)}, f32[4,3,1,2,32,256]{5,4,3,2,1,0:T(8,128)S(1)}, u32[]{:S(2)}) copy-start(f32[4,3,1,2,32,256]{5,4,3,2,1,0:T(8,128)S(1)} %pad_maximum_fusion.refs_10_) | copy-start | bytes 2359300
  34.1 33.4 %collective-permute-start.12 = (f32[4,3,1,2,32,256]{5,4,3,2,1,0:T(8,128)S(1)}, f32[4,3,1,2,32,256]{5,4,3,2,1,0:T(8,128)S(1)}, u32[]{:S(2)}, u32[]{:S(2)}) collective-permute-start(f32[4,3,1,2,32,256]{5,4,3,2,1,0:T(8,128)S(1)} %pad_maximum_fusion.refs_10_), channel_id=1, source_target_pairs={{0,4},{4,0},{8,12},{12,8},{16,20},{20,16},{24,28},{28,24},{1,5},{5... | collective-permute-start | bytes 2359304 | tf_op jit(solution)/shard_map/ppermute | solution.py:31
  35.4 32.1 %copy-start.1 = (f32[4,3,1,2,32,256]{5,4,3,2,1,0:T(8,128)}, f32[4,3,1,2,32,256]{5,4,3,2,1,0:T(8,128)S(1)}, u32[]{:S(2)}) copy-start(f32[4,3,1,2,32,256]{5,4,3,2,1,0:T(8,128)S(1)} %pad_maximum_fusion.1.refs_12_) | copy-start | bytes 2359300
  35.4 32.1 %collective-permute-start.15 = (f32[4,3,1,2,32,256]{5,4,3,2,1,0:T(8,128)S(1)}, f32[4,3,1,2,32,256]{5,4,3,2,1,0:T(8,128)}, u32[]{:S(2)}, u32[]{:S(2)}) collective-permute-start(f32[4,3,1,2,32,256]{5,4,3,2,1,0:T(8,128)S(1)} %pad_maximum_fusion.1.refs_12_), channel_id=1, source_target_pairs={{0,4},{4,0},{8,12},{12,8},{16,20},{20,16},{24,28},{28,24},{1,5},{5... | collective-permute-start | bytes 2359304 | tf_op jit(solution)/shard_map/ppermute | solution.py:31
  35.5 8.8 %collective-permute-start.2 = (bf16[2,256,256]{2,1,0:T(8,128)(2,1)S(1)}, bf16[2,256,256]{2,1,0:T(8,128)(2,1)}, u32[]{:S(2)}, u32[]{:S(2)}) collective-permute-start(bf16[2,256,256]{2,1,0:T(8,128)(2,1)S(1)} %convert_element_type.66.refs_1_), channel_id=1, source_target_pairs={{0,3},{1,0},{2,1},{3,2},{4,7},{5,4},{6,5},{7,6},{8,11},{9,8},{10,9... | collective-permute-start | bytes 786440 | tf_op jit(solution)/shard_map/ppermute | solution.py:26
  36.4 25.4 %collective-permute-start.1 = (bf16[2,256,256]{2,1,0:T(8,128)(2,1)S(1)}, bf16[2,256,256]{2,1,0:T(8,128)(2,1)}, u32[]{:S(2)}, u32[]{:S(2)}) collective-permute-start(bf16[2,256,256]{2,1,0:T(8,128)(2,1)S(1)} %convert_element_type.66.refs_1_), channel_id=1, source_target_pairs={{0,2},{1,3},{2,0},{3,1},{4,6},{5,7},{6,4},{7,5},{8,10},{9,11},{10,... | collective-permute-start | bytes 786440 | tf_op jit(solution)/shard_map/ppermute | solution.py:26
  38.0 29.5 %copy-start.8 = (bf16[2,256,256]{2,1,0:T(8,128)(2,1)}, bf16[2,256,256]{2,1,0:T(8,128)(2,1)S(1)}, u32[]{:S(2)}) copy-start(bf16[2,256,256]{2,1,0:T(8,128)(2,1)S(1)} %collective-permute-done.3.refs_5_) | copy-start | bytes 786436
  38.0 25.1 %collective-permute-start = (bf16[2,256,256]{2,1,0:T(8,128)(2,1)S(1)}, bf16[2,256,256]{2,1,0:T(8,128)(2,1)}, u32[]{:S(2)}, u32[]{:S(2)}) collective-permute-start(bf16[2,256,256]{2,1,0:T(8,128)(2,1)S(1)} %convert_element_type.66.refs_1_), channel_id=1, source_target_pairs={{0,1},{1,2},{2,3},{3,0},{4,5},{5,6},{6,7},{7,4},{8,9},{9,10},{10,1... | collective-permute-start | bytes 786440 | tf_op jit(solution)/shard_map/ppermute | solution.py:26
  44.3 21.5 %collective-permute-start.6 = (bf16[2,256,256]{2,1,0:T(8,128)(2,1)}, bf16[2,256,256]{2,1,0:T(8,128)(2,1)}, u32[]{:S(2)}, u32[]{:S(2)}) collective-permute-start(bf16[2,256,256]{2,1,0:T(8,128)(2,1)} %collective-permute-done.2.refs_4_), channel_id=1, source_target_pairs={{4,0},{8,4},{12,8},{16,12},{20,16},{24,20},{28,24},{5,1},{9,5},{13... | collective-permute-start | bytes 786440 | tf_op jit(solution)/shard_map/ppermute | solution.py:21
  61.8 4.0 %collective-permute-start.5 = (bf16[2,256,256]{2,1,0:T(8,128)(2,1)}, bf16[2,256,256]{2,1,0:T(8,128)(2,1)}, u32[]{:S(2)}, u32[]{:S(2)}) collective-permute-start(bf16[2,256,256]{2,1,0:T(8,128)(2,1)} %collective-permute-done.1.refs_3_), channel_id=1, source_target_pairs={{4,0},{8,4},{12,8},{16,12},{20,16},{24,20},{28,24},{5,1},{9,5},{13... | collective-permute-start | bytes 786440 | tf_op jit(solution)/shard_map/ppermute | solution.py:21
  63.1 4.4 %collective-permute-start.4 = (bf16[2,256,256]{2,1,0:T(8,128)(2,1)}, bf16[2,256,256]{2,1,0:T(8,128)(2,1)}, u32[]{:S(2)}, u32[]{:S(2)}) collective-permute-start(bf16[2,256,256]{2,1,0:T(8,128)(2,1)} %collective-permute-done.refs_2_), channel_id=1, source_target_pairs={{4,0},{8,4},{12,8},{16,12},{20,16},{24,20},{28,24},{5,1},{9,5},{13... | collective-permute-start | bytes 786440 | tf_op jit(solution)/shard_map/ppermute | solution.py:21
  67.5 0.9 copy-start.6
  90.7 15.1 %collective-permute-start.21 = (bf16[4,17,32,256]{3,2,1,0:T(8,128)(2,1)}, bf16[4,17,32,256]{3,2,1,0:T(8,128)(2,1)S(1)}, u32[]{:S(2)}, u32[]{:S(2)}) collective-permute-start(bf16[4,17,32,256]{3,2,1,0:T(8,128)(2,1)} %get-tuple-element.11), channel_id=1, source_target_pairs={{0,4},{4,0},{8,12},{12,8},{16,20},{20,16},{24,28},{28,24},{1,5},{5... | collective-permute-start | bytes 3342344 | tf_op jit(solution)/shard_map/ppermute | solution.py:31
  95.7 25.8 %collective-permute-start.16 = (bf16[4,2,256,256]{3,2,1,0:T(8,128)(2,1)}, bf16[4,2,256,256]{3,2,1,0:T(8,128)(2,1)S(1)}, u32[]{:S(2)}, u32[]{:S(2)}) collective-permute-start(bf16[4,2,256,256]{3,2,1,0:T(8,128)(2,1)} %get-tuple-element.8), channel_id=1, source_target_pairs={{0,4},{4,8},{8,12},{12,16},{16,20},{20,24},{24,28},{1,5},{5,9},{9,... | collective-permute-start | bytes 3145736 | tf_op jit(solution)/shard_map/ppermute | solution.py:21
  97.7 5.1 %collective-permute-start.20 = (s32[17]{0:T(128)S(1)}, s32[17]{0:T(128)S(1)}, u32[]{:S(2)}, u32[]{:S(2)}) collective-permute-start(s32[17]{0:T(128)S(1)} %pad_add_fusion.1), channel_id=1, source_target_pairs={{0,4},{4,8},{8,12},{12,16},{16,20},{20,24},{24,28},{1,5},{5,9},{9,... | collective-permute-start | bytes 212 | tf_op jit(solution)/shard_map/ppermute | solution.py:21
  107.9 13.5 %copy-start.3 = (bf16[4,2,256,256]{3,2,1,0:T(8,128)(2,1)S(1)}, bf16[4,2,256,256]{3,2,1,0:T(8,128)(2,1)}, u32[]{:S(2)}) copy-start(bf16[4,2,256,256]{3,2,1,0:T(8,128)(2,1)} %get-tuple-element.7) | copy-start | bytes 3145732
  108.0 19.4 %collective-permute-start.22 = (bf16[17,32,256]{2,1,0:T(8,128)(2,1)S(1)}, bf16[17,32,256]{2,1,0:T(8,128)(2,1)S(1)}, u32[]{:S(2)}, u32[]{:S(2)}) collective-permute-start(bf16[17,32,256]{2,1,0:T(8,128)(2,1)S(1)} %get-tuple-element.18), channel_id=1, source_target_pairs={{0,8},{4,12},{8,0},{12,4},{16,24},{20,28},{24,16},{28,20},{1,9},{5... | collective-permute-start | bytes 835592 | tf_op jit(solution)/shard_map/ppermute | solution.py:31
  119.9 10.4 %collective-permute-start.24 = (bf16[17,32,256]{2,1,0:T(8,128)(2,1)S(1)}, bf16[17,32,256]{2,1,0:T(8,128)(2,1)S(1)}, u32[]{:S(2)}, u32[]{:S(2)}) collective-permute-start(bf16[17,32,256]{2,1,0:T(8,128)(2,1)S(1)} %get-tuple-element.19), channel_id=1, source_target_pairs={{0,24},{4,28},{8,16},{12,20},{16,8},{20,12},{24,0},{28,4},{1,25},{... | collective-permute-start | bytes 835592 | tf_op jit(solution)/shard_map/ppermute | solution.py:31
  121.2 11.9 %collective-permute-start.23 = (bf16[17,32,256]{2,1,0:T(8,128)(2,1)S(1)}, bf16[17,32,256]{2,1,0:T(8,128)(2,1)S(1)}, u32[]{:S(2)}, u32[]{:S(2)}) collective-permute-start(bf16[17,32,256]{2,1,0:T(8,128)(2,1)S(1)} %get-tuple-element.20), channel_id=1, source_target_pairs={{0,16},{4,20},{8,24},{12,28},{16,0},{20,4},{24,8},{28,12},{1,17},{... | collective-permute-start | bytes 835592 | tf_op jit(solution)/shard_map/ppermute | solution.py:31
  133.3 16.7 %copy-start.5 = (f32[256,256]{1,0:T(8,128)S(1)}, f32[256,256]{1,0:T(8,128)}, u32[]{:S(2)}) copy-start(f32[256,256]{1,0:T(8,128)} %illumination.1) | copy-start | bytes 786436
  133.4 7.8 %collective-permute-start.25 = (bf16[5,32,256]{2,1,0:T(8,128)(2,1)S(1)}, bf16[5,32,256]{2,1,0:T(8,128)(2,1)S(1)}, u32[]{:S(2)}, u32[]{:S(2)}) collective-permute-start(bf16[5,32,256]{2,1,0:T(8,128)(2,1)S(1)} %get-tuple-element.28), channel_id=1, source_target_pairs={{0,1},{1,2},{2,3},{3,0},{4,5},{5,6},{6,7},{7,4},{8,9},{9,10},{10,1... | collective-permute-start | bytes 245768 | tf_op jit(solution)/shard_map/ppermute | solution.py:26
  133.4 12.5 %collective-permute-start.26 = (bf16[5,32,256]{2,1,0:T(8,128)(2,1)S(1)}, bf16[5,32,256]{2,1,0:T(8,128)(2,1)S(1)}, u32[]{:S(2)}, u32[]{:S(2)}) collective-permute-start(bf16[5,32,256]{2,1,0:T(8,128)(2,1)S(1)} %get-tuple-element.29), channel_id=1, source_target_pairs={{0,2},{1,3},{2,0},{3,1},{4,6},{5,7},{6,4},{7,5},{8,10},{9,11},{10,... | collective-permute-start | bytes 245768 | tf_op jit(solution)/shard_map/ppermute | solution.py:26
  133.9 12.4 %collective-permute-start.27 = (bf16[5,32,256]{2,1,0:T(8,128)(2,1)S(1)}, bf16[5,32,256]{2,1,0:T(8,128)(2,1)S(1)}, u32[]{:S(2)}, u32[]{:S(2)}) collective-permute-start(bf16[5,32,256]{2,1,0:T(8,128)(2,1)S(1)} %concatenate.75), channel_id=1, source_target_pairs={{0,3},{1,0},{2,1},{3,2},{4,7},{5,4},{6,5},{7,6},{8,11},{9,8},{10,9... | collective-permute-start | bytes 245768 | tf_op jit(solution)/shard_map/ppermute | solution.py:26
  137.3 12.4 %collective-permute-start.17 = (bf16[2,256,256]{2,1,0:T(8,128)(2,1)S(1)}, bf16[2,256,256]{2,1,0:T(8,128)(2,1)S(1)}, u32[]{:S(2)}, u32[]{:S(2)}) collective-permute-start(bf16[2,256,256]{2,1,0:T(8,128)(2,1)S(1)} %get-tuple-element.21), channel_id=1, source_target_pairs={{0,1},{1,2},{2,3},{3,0},{4,5},{5,6},{6,7},{7,4},{8,9},{9,10},{10,1... | collective-permute-start | bytes 786440 | tf_op jit(solution)/shard_map/ppermute | solution.py:26
  137.9 14.7 %collective-permute-start.19 = (bf16[2,256,256]{2,1,0:T(8,128)(2,1)S(1)}, bf16[2,256,256]{2,1,0:T(8,128)(2,1)S(1)}, u32[]{:S(2)}, u32[]{:S(2)}) collective-permute-start(bf16[2,256,256]{2,1,0:T(8,128)(2,1)S(1)} %get-tuple-element.22), channel_id=1, source_target_pairs={{0,3},{1,0},{2,1},{3,2},{4,7},{5,4},{6,5},{7,6},{8,11},{9,8},{10,9... | collective-permute-start | bytes 786440 | tf_op jit(solution)/shard_map/ppermute | solution.py:26
  141.2 24.4 %collective-permute-start.18 = (bf16[2,256,256]{2,1,0:T(8,128)(2,1)S(1)}, bf16[2,256,256]{2,1,0:T(8,128)(2,1)S(1)}, u32[]{:S(2)}, u32[]{:S(2)}) collective-permute-start(bf16[2,256,256]{2,1,0:T(8,128)(2,1)S(1)} %get-tuple-element.23), channel_id=1, source_target_pairs={{0,2},{1,3},{2,0},{3,1},{4,6},{5,7},{6,4},{7,5},{8,10},{9,11},{10,... | collective-permute-start | bytes 786440 | tf_op jit(solution)/shard_map/ppermute | solution.py:26
  146.4 20.2 %copy-start.7 = (f32[4,32,256]{2,1,0:T(8,128)}, f32[4,32,256]{2,1,0:T(8,128)S(1)}, u32[]{:S(2)}) copy-start(f32[4,32,256]{2,1,0:T(8,128)S(1)} %slice_divide_fusion.refs_0_) | copy-start | bytes 393220
  146.4 6.2 %collective-permute-start.30 = (f32[4,32,256]{2,1,0:T(8,128)S(1)}, f32[4,32,256]{2,1,0:T(8,128)S(1)}, u32[]{:S(2)}, u32[]{:S(2)}) collective-permute-start(f32[4,32,256]{2,1,0:T(8,128)S(1)} %slice_divide_fusion.refs_0_), channel_id=1, source_target_pairs={{0,24},{4,28},{8,16},{12,20},{16,8},{20,12},{24,0},{28,4},{1,25},{... | collective-permute-start | bytes 393224 | tf_op jit(solution)/shard_map/ppermute | solution.py:31
  146.5 6.6 %collective-permute-start.29 = (f32[4,32,256]{2,1,0:T(8,128)S(1)}, f32[4,32,256]{2,1,0:T(8,128)S(1)}, u32[]{:S(2)}, u32[]{:S(2)}) collective-permute-start(f32[4,32,256]{2,1,0:T(8,128)S(1)} %slice_divide_fusion.refs_0_), channel_id=1, source_target_pairs={{0,16},{4,20},{8,24},{12,28},{16,0},{20,4},{24,8},{28,12},{1,17},{... | collective-permute-start | bytes 393224 | tf_op jit(solution)/shard_map/ppermute | solution.py:31
  149.7 5.0 %collective-permute-start.28 = (f32[4,32,256]{2,1,0:T(8,128)S(1)}, f32[4,32,256]{2,1,0:T(8,128)S(1)}, u32[]{:S(2)}, u32[]{:S(2)}) collective-permute-start(f32[4,32,256]{2,1,0:T(8,128)S(1)} %slice_divide_fusion.refs_0_), channel_id=1, source_target_pairs={{0,8},{4,12},{8,0},{12,4},{16,24},{20,28},{24,16},{28,20},{1,9},{5... | collective-permute-start | bytes 393224 | tf_op jit(solution)/shard_map/ppermute | solution.py:31
  152.6 14.0 %collective-permute-start.31 = (f32[4,32,256]{2,1,0:T(8,128)S(1)}, f32[4,32,256]{2,1,0:T(8,128)S(1)}, u32[]{:S(2)}, u32[]{:S(2)}) collective-permute-start(f32[4,32,256]{2,1,0:T(8,128)S(1)} %slice_divide_fusion.refs_0_), channel_id=1, source_target_pairs={{0,4},{4,0},{8,12},{12,8},{16,20},{20,16},{24,28},{28,24},{1,5},{5... | collective-permute-start | bytes 393224 | tf_op jit(solution)/shard_map/ppermute | solution.py:31
  152.6 14.0 %copy-start.9 = (f32[4,32,256]{2,1,0:T(8,128)}, f32[4,32,256]{2,1,0:T(8,128)S(1)}, u32[]{:S(2)}) copy-start(f32[4,32,256]{2,1,0:T(8,128)S(1)} %collective-permute-done.30.refs_3_) | copy-start | bytes 393220
  152.6 14.0 %collective-permute-start.34 = (f32[4,32,256]{2,1,0:T(8,128)S(1)}, f32[4,32,256]{2,1,0:T(8,128)S(1)}, u32[]{:S(2)}, u32[]{:S(2)}) collective-permute-start(f32[4,32,256]{2,1,0:T(8,128)S(1)} %collective-permute-done.30.refs_3_), channel_id=1, source_target_pairs={{0,4},{4,0},{8,12},{12,8},{16,20},{20,16},{24,28},{28,24},{1,5},{5... | collective-permute-start | bytes 393224 | tf_op jit(solution)/shard_map/ppermute | solution.py:31
  153.1 13.5 %copy-start.10 = (f32[4,32,256]{2,1,0:T(8,128)}, f32[4,32,256]{2,1,0:T(8,128)S(1)}, u32[]{:S(2)}) copy-start(f32[4,32,256]{2,1,0:T(8,128)S(1)} %collective-permute-done.29.refs_2_) | copy-start | bytes 393220
  153.1 13.5 %collective-permute-start.33 = (f32[4,32,256]{2,1,0:T(8,128)S(1)}, f32[4,32,256]{2,1,0:T(8,128)S(1)}, u32[]{:S(2)}, u32[]{:S(2)}) collective-permute-start(f32[4,32,256]{2,1,0:T(8,128)S(1)} %collective-permute-done.29.refs_2_), channel_id=1, source_target_pairs={{0,4},{4,0},{8,12},{12,8},{16,20},{20,16},{24,28},{28,24},{1,5},{5... | collective-permute-start | bytes 393224 | tf_op jit(solution)/shard_map/ppermute | solution.py:31
  154.6 12.0 %copy-start.11 = (f32[4,32,256]{2,1,0:T(8,128)}, f32[4,32,256]{2,1,0:T(8,128)S(1)}, u32[]{:S(2)}) copy-start(f32[4,32,256]{2,1,0:T(8,128)S(1)} %collective-permute-done.28.refs_1_) | copy-start | bytes 393220
  154.6 12.0 %collective-permute-start.32 = (f32[4,32,256]{2,1,0:T(8,128)S(1)}, f32[4,32,256]{2,1,0:T(8,128)S(1)}, u32[]{:S(2)}, u32[]{:S(2)}) collective-permute-start(f32[4,32,256]{2,1,0:T(8,128)S(1)} %collective-permute-done.28.refs_1_), channel_id=1, source_target_pairs={{0,4},{4,0},{8,12},{12,8},{16,20},{20,16},{24,28},{28,24},{1,5},{5... | collective-permute-start | bytes 393224 | tf_op jit(solution)/shard_map/ppermute | solution.py:31
  (5 other events, 3.2 us)

commit v3 on v2

--- a/solution.py
+++ b/solution.py
@@ -163,16 +163,17 @@
                 num[1] += probe[m, 0] * ni - probe[m, 1] * nr
                 grads[2 * m] += win[0] * nr + win[1] * ni
                 grads[2 * m + 1] += win[0] * ni - win[1] * nr
+            below = lax.broadcasted_iota(jnp.int32, (width, width), 0) < row + width - band
             for ch in range(2):
                 add_window(buffer, ch, num[ch], row, col, cols)
+                rim_out[k, ch] = jnp.where(
+                    below, pltpu.roll(num[ch], row + width - band, 0), 0.0
+                ).astype(bf16)
             return carry
 
         lax.fori_loop(0, slots, one_slot, 0)
-        for d in range(tiles):
-            for ch in range(2):
-                at = pl.multiple_of((tile_at + d) % tiles * band, band)
-                main_out[d, ch] = buffer[ch, 0:band, pl.ds(at, band)].astype(bf16)
-                rim_out[d, ch] = buffer[ch, band : 2 * band, pl.ds(at, band)].astype(bf16)
+        for ch in range(2):
+            main_out[ch] = buffer[ch, 0:band].astype(bf16)
         for k in range(spread):
             at = pl.multiple_of(((scan_at % spread) ^ k) * part, part)
             out = odd_out if k % 2 else even_out
@@ -182,6 +183,29 @@
                     value = grads[first + ch, pl.ds(at, part)]
                     out[k // 2, d * 2 * local + ch] = value.astype(out.dtype)
             out[k // 2, 2 * modes] = weight[pl.ds(at, part)].astype(out.dtype)
+
+    return body
+
+
+def rim_kernel(tiles, slots, width, band):
+    cols = tiles * band
+
+    def body(meta, above, main, lower, *rest):
+        outs, buffer = rest[:tiles], rest[tiles]
+        buffer[...] = main[...].astype(f32)
+        for k in range(slots):
+            col = above[2 * (meta[1] + tiles * k) + 1]
+            col_at = pl.multiple_of(jnp.minimum(col // 128 * 128, cols - width - 128), 128)
+            for ch in range(2):
+                value = lower[k, ch].astype(f32)
+                value = jnp.concatenate([value, jnp.zeros((width, 128), f32)], 1)
+                buffer[ch, 0:width, pl.ds(col_at, width + 128)] += pltpu.roll(
+                    value, col - col_at, 1
+                )
+        for d in range(tiles):
+            at = pl.multiple_of((meta[1] + d) % tiles * band, band)
+            for ch in range(2):
+                outs[d][ch] = buffer[ch, :, pl.ds(at, band)].astype(outs[d].dtype)
 
     return body
 
@@ -262,8 +286,8 @@
     main, rim, power, odd, even = pl.pallas_call(
         main_kernel(tiles, slots, modes, width, band, spread, part),
         out_shape=(
-            jax.ShapeDtypeStruct((tiles, 2, band, band), bf16),
-            jax.ShapeDtypeStruct((tiles, 2, band, band), bf16),
+            jax.ShapeDtypeStruct((2, band, tiles * band), bf16),
+            jax.ShapeDtypeStruct((slots, 2, width, width), bf16),
             jax.ShapeDtypeStruct((width, width), f32),
             jax.ShapeDtypeStruct((spread // 2, 2 * modes + 1, part, width), bf16),
             jax.ShapeDtypeStruct((spread // 2, 2 * modes + 1, part, width), f32),
@@ -297,10 +321,19 @@
         minus,
     )
 
-    share = main.astype(f32) + shifted(rim, "scan", 1).astype(f32)
-    totals = share[0]
+    lower = shifted(rim, "scan", 1)
+    kept, *sent = pl.pallas_call(
+        rim_kernel(tiles, slots, width, band),
+        out_shape=(jax.ShapeDtypeStruct((2, band, band), f32),)
+        + (jax.ShapeDtypeStruct((2, band, band), bf16),) * (tiles - 1),
+        in_specs=[smem, smem, vmem, vmem],
+        out_specs=(vmem,) * tiles,
+        scratch_shapes=[pltpu.VMEM((2, band, tiles * band), f32)],
+        name="rims",
+    )(meta, above, main, lower)
+    totals = kept
     for d in range(1, tiles):
-        totals = totals + rotated(share[d].astype(bf16), "tile", d).astype(f32)
+        totals = totals + rotated(sent[d - 1], "tile", d).astype(f32)
 
     illumination = pl.pallas_call(
         illum_kernel(slot_count, width, band),

time: 171 us -> 169 us (0.988)
  the two profiles are of different devices: /device:TPU:0 before, /device:TPU:21 now
where the time goes in v3:
time: 169 us
  waiting for transfers between devices  72.6 us (43%)
  starting transfers between devices  53.6 us (32%)
  Pallas kernels  30.6 us (18%)
  other arithmetic  5.38 us (3%)
  local copies, waits for them, and re-layouts  4.81 us (3%)
  between operations  1.69 us (1%)
    ppermute x12, waiting for transfers between devices, rotated(): lax.ppermute(value, axis, [(i, (i + steps) % count) for i in range(count)])  40.2 us
    ppermute x17, waiting for transfers between devices, swapped(): return lax.ppermute(value, axis, pairs)  25.3 us
    pallas_call x1, Pallas kernels, update(): pl.pallas_call(main_kernel(tiles, slots, modes, width, band, spread, part...  22.3 us
    ppermute x17, starting transfers between devices, swapped(): return lax.ppermute(value, axis, pairs)  21.4 us
    ppermute x6, starting transfers between devices, shifted(): return lax.ppermute(value, axis, pairs)  19.4 us
    ppermute x12, starting transfers between devices, rotated(): lax.ppermute(value, axis, [(i, (i + steps) % count) for i in range(count)])  12.8 us
    ppermute x6, waiting for transfers between devices, shifted(): return lax.ppermute(value, axis, pairs)  7.07 us
    unnamed x39, local copies, waits for them, and re-layouts  3.63 us
  transfers between devices with their start and end apart: 35, of which 18 were waited for; matrix products, arithmetic and copies ran while one was open for 2% of the time, Pallas kernels for 4%

profile of v3, /device:TPU:21, one launch (start us, length us, event | category | flops | bytes accessed | tf_op | source)
XLA Modules:
  0.0 168.7 jit_solution(1856581767329196069)
XLA Ops:
  0.7 1.0 constant_dynamic-slice_fusion
  1.9 3.2 %collective-permute-start.9 = (f32[2,2,32,256]{3,2,1,0:T(8,128)S(1)}, f32[2,2,32,256]{3,2,1,0:T(8,128)S(1)}, u32[]{:S(2)}, u32[]{:S(2)}) collective-permute-start(f32[2,2,32,256]{3,2,1,0:T(8,128)S(1)} %constant_dynamic-slice_fusion), channel_id=1, source_target_pairs={{0,2},{1,3},{2,0},{3,1},{4,6},{5,7},{6,4},{7,5},{8,10},{9,11},{10,... | collective-permute-start | bytes 393224 | tf_op jit(solution)/shard_map/ppermute | solution.py:26
  5.1 1.0 collective-permute-done.10
  6.1 7.0 %collective-permute-done.9 = f32[2,2,32,256]{3,2,1,0:T(8,128)S(1)} collective-permute-done((f32[2,2,32,256]{3,2,1,0:T(8,128)S(1)}, f32[2,2,32,256]{3,2,1,0:T(8,128)S(1)}, u32[]{:S(2)}, u32[]{:S(2)}) %collective-permute-start.9) | collective-permute-done | bytes 131104 | tf_op jit(solution)/shard_map/ppermute | solution.py:26
  13.0 3.0 %collective-permute-done.8 = f32[2,2,32,256]{3,2,1,0:T(8,128)S(1)} collective-permute-done((f32[2,2,32,256]{3,2,1,0:T(8,128)S(1)}, f32[2,2,32,256]{3,2,1,0:T(8,128)S(1)}, u32[]{:S(2)}, u32[]{:S(2)}) %collective-permute-start.8) | collective-permute-done | bytes 131104 | tf_op jit(solution)/shard_map/ppermute | solution.py:26
  16.1 1.3 collective-permute-start.11
  17.6 3.8 %collective-permute-done.11 = f32[1,3,1,2,32,256]{5,4,3,2,1,0:T(8,128)S(1)} collective-permute-done((f32[1,3,1,2,32,256]{5,4,3,2,1,0:T(8,128)S(1)}, f32[1,3,1,2,32,256]{5,4,3,2,1,0:T(8,128)S(1)}, u32[]{:S(2)}, u32[]{:S(2)}) %collective-permute-start.11) | collective-permute-done | bytes 196640 | tf_op jit(solution)/shard_map/ppermute | solution.py:31
  21.7 0.6 collective-permute-done.14
  22.3 0.7 collective-permute-start.15
  23.0 4.5 %collective-permute-start.4 = (bf16[2,256,256]{2,1,0:T(8,128)(2,1)S(1)}, bf16[2,256,256]{2,1,0:T(8,128)(2,1)S(1)}, u32[]{:S(2)}, u32[]{:S(2)}) collective-permute-start(bf16[2,256,256]{2,1,0:T(8,128)(2,1)S(1)} %convert_element_type.48.refs_1_), channel_id=1, source_target_pairs={{4,0},{8,4},{12,8},{16,12},{20,16},{24,20},{28,24},{5,1},{9,5},{13... | collective-permute-start | bytes 786440 | tf_op jit(solution)/shard_map/ppermute | solution.py:21
  27.6 2.6 %collective-permute-done.12 = f32[2,3,1,2,32,256]{5,4,3,2,1,0:T(8,128)S(1)} collective-permute-done((f32[2,3,1,2,32,256]{5,4,3,2,1,0:T(8,128)S(1)}, f32[2,3,1,2,32,256]{5,4,3,2,1,0:T(8,128)S(1)}, u32[]{:S(2)}, u32[]{:S(2)}) %collective-permute-start.12) | collective-permute-done | bytes 393248 | tf_op jit(solution)/shard_map/ppermute | solution.py:31
  30.3 2.9 %collective-permute-start.13 = (f32[4,3,1,2,32,256]{5,4,3,2,1,0:T(8,128)S(1)}, f32[4,3,1,2,32,256]{5,4,3,2,1,0:T(8,128)S(1)}, u32[]{:S(2)}, u32[]{:S(2)}) collective-permute-start(f32[4,3,1,2,32,256]{5,4,3,2,1,0:T(8,128)S(1)} %pad_maximum_fusion.refs_10_), channel_id=1, source_target_pairs={{0,4},{4,0},{8,12},{12,8},{16,20},{20,16},{24,28},{28,24},{1,5},{5... | collective-permute-start | bytes 2359304 | tf_op jit(solution)/shard_map/ppermute | solution.py:31
  33.3 0.8 collective-permute-start.16
  34.1 1.2 collective-permute-start.2
  35.3 0.8 collective-permute-done.4.refs_5_
  36.0 5.9 %collective-permute-done.3.refs_4_ = bf16[2,256,256]{2,1,0:T(8,128)(2,1)} collective-permute-done((bf16[2,256,256]{2,1,0:T(8,128)(2,1)S(1)}, bf16[2,256,256]{2,1,0:T(8,128)(2,1)}, u32[]{:S(2)}, u32[]{:S(2)}) %collective-permute-start.3) | collective-permute-done | bytes 262176 | tf_op jit(solution)/shard_map/ppermute | solution.py:26
  41.9 3.4 %collective-permute-start.7 = (bf16[2,256,256]{2,1,0:T(8,128)(2,1)}, bf16[2,256,256]{2,1,0:T(8,128)(2,1)}, u32[]{:S(2)}, u32[]{:S(2)}) collective-permute-start(bf16[2,256,256]{2,1,0:T(8,128)(2,1)} %collective-permute-done.3.refs_4_), channel_id=1, source_target_pairs={{4,0},{8,4},{12,8},{16,12},{20,16},{24,20},{28,24},{5,1},{9,5},{13... | collective-permute-start | bytes 786440 | tf_op jit(solution)/shard_map/ppermute | solution.py:21
  45.3 11.5 %collective-permute-done.2.refs_3_ = bf16[2,256,256]{2,1,0:T(8,128)(2,1)} collective-permute-done((bf16[2,256,256]{2,1,0:T(8,128)(2,1)S(1)}, bf16[2,256,256]{2,1,0:T(8,128)(2,1)}, u32[]{:S(2)}, u32[]{:S(2)}) %collective-permute-start.2) | collective-permute-done | bytes 262176 | tf_op jit(solution)/shard_map/ppermute | solution.py:26
  56.8 2.5 %collective-permute-start.6 = (bf16[2,256,256]{2,1,0:T(8,128)(2,1)}, bf16[2,256,256]{2,1,0:T(8,128)(2,1)}, u32[]{:S(2)}, u32[]{:S(2)}) collective-permute-start(bf16[2,256,256]{2,1,0:T(8,128)(2,1)} %collective-permute-done.2.refs_3_), channel_id=1, source_target_pairs={{4,0},{8,4},{12,8},{16,12},{20,16},{24,20},{28,24},{5,1},{9,5},{13... | collective-permute-start | bytes 786440 | tf_op jit(solution)/shard_map/ppermute | solution.py:21
  59.3 3.2 %collective-permute-start.5 = (bf16[2,256,256]{2,1,0:T(8,128)(2,1)}, bf16[2,256,256]{2,1,0:T(8,128)(2,1)}, u32[]{:S(2)}, u32[]{:S(2)}) collective-permute-start(bf16[2,256,256]{2,1,0:T(8,128)(2,1)} %collective-permute-done.1.refs_2_), channel_id=1, source_target_pairs={{4,0},{8,4},{12,8},{16,12},{20,16},{24,20},{28,24},{5,1},{9,5},{13... | collective-permute-start | bytes 786440 | tf_op jit(solution)/shard_map/ppermute | solution.py:21
  63.4 0.6 pad_add_fusion.refs_0_.meta
  64.0 0.7 collective-permute-done.6.refs_7_
  64.8 2.8 %collective-permute-done.5.refs_6_ = bf16[2,256,256]{2,1,0:T(8,128)(2,1)} collective-permute-done((bf16[2,256,256]{2,1,0:T(8,128)(2,1)}, bf16[2,256,256]{2,1,0:T(8,128)(2,1)}, u32[]{:S(2)}, u32[]{:S(2)}) %collective-permute-start.5) | collective-permute-done | bytes 262176 | tf_op jit(solution)/shard_map/ppermute | solution.py:21
  67.6 0.9 copy-done.5
  68.5 22.3 %update.1 = (bf16[2,256,1024]{2,1,0:T(8,128)(2,1)}, bf16[2,2,256,256]{3,2,1,0:T(8,128)(2,1)}, f32[256,256]{1,0:T(8,128)}, bf16[4,17,32,256]{3,2,1,0:T(8,128)(2,1)}, f32[4,17,32,256]{3,2,1,0:T(8,128)}) custom-call(s32[19]{0:T(128)} %pad_add_fusion.refs_0_.meta, bf16[2,256,256]{2,1,0:T(8,128)(2,1)} %copy-done.3, ...), custom_call_target="tpu_custom_call" | custom-call | tf_op jit(solution)/shard_map/update/pallas_call | solution.py:286
  90.8 2.9 %collective-permute-done.21 = bf16[4,17,32,256]{3,2,1,0:T(8,128)(2,1)S(1)} collective-permute-done((bf16[4,17,32,256]{3,2,1,0:T(8,128)(2,1)}, bf16[4,17,32,256]{3,2,1,0:T(8,128)(2,1)S(1)}, u32[]{:S(2)}, u32[]{:S(2)}) %collective-permute-start.21) | collective-permute-done | bytes 1114144 | tf_op jit(solution)/shard_map/ppermute | solution.py:31
  93.8 2.2 %fusion.8 = (bf16[4,17,32,256]{3,2,1,0:T(8,128)(2,1)S(1)}, f32[4,17,32,256]{3,2,1,0:T(8,128)S(1)}) fusion(f32[4,17,32,256]{3,2,1,0:T(8,128)} %get-tuple-element.18, bf16[4,17,32,256]{3,2,1,0:T(8,128)(2,1)S(1)} %collective-permute-done.21), kind=kLoop, calls=%fused_computation.28 | loop fusion | flops 1671168 | bytes 6684672 | tf_op jit(solution)/shard_map/convert.9
  96.1 2.5 %collective-permute-start.24 = (bf16[17,32,256]{2,1,0:T(8,128)(2,1)S(1)}, bf16[17,32,256]{2,1,0:T(8,128)(2,1)S(1)}, u32[]{:S(2)}, u32[]{:S(2)}) collective-permute-start(bf16[17,32,256]{2,1,0:T(8,128)(2,1)S(1)} %get-tuple-element.25), channel_id=1, source_target_pairs={{0,24},{4,28},{8,16},{12,20},{16,8},{20,12},{24,0},{28,4},{1,25},{... | collective-permute-start | bytes 835592 | tf_op jit(solution)/shard_map/ppermute | solution.py:31
  98.8 3.8 %collective-permute-start.17 = (bf16[2,2,256,256]{3,2,1,0:T(8,128)(2,1)S(1)}, bf16[2,2,256,256]{3,2,1,0:T(8,128)(2,1)S(1)}, u32[]{:S(2)}, u32[]{:S(2)}) collective-permute-start(bf16[2,2,256,256]{3,2,1,0:T(8,128)(2,1)S(1)} %copy-done.18), channel_id=1, source_target_pairs={{0,4},{4,8},{8,12},{12,16},{16,20},{20,24},{24,28},{1,5},{5,9},{9,... | collective-permute-start | bytes 1572872 | tf_op jit(solution)/shard_map/ppermute | solution.py:21
  102.7 1.5 collective-permute-done.22
  104.2 7.3 %collective-permute-done.24 = bf16[17,32,256]{2,1,0:T(8,128)(2,1)S(1)} collective-permute-done((bf16[17,32,256]{2,1,0:T(8,128)(2,1)S(1)}, bf16[17,32,256]{2,1,0:T(8,128)(2,1)S(1)}, u32[]{:S(2)}, u32[]{:S(2)}) %collective-permute-start.24) | collective-permute-done | bytes 278560 | tf_op jit(solution)/shard_map/ppermute | solution.py:31
  111.5 6.6 %collective-permute-done.23 = bf16[17,32,256]{2,1,0:T(8,128)(2,1)S(1)} collective-permute-done((bf16[17,32,256]{2,1,0:T(8,128)(2,1)S(1)}, bf16[17,32,256]{2,1,0:T(8,128)(2,1)S(1)}, u32[]{:S(2)}, u32[]{:S(2)}) %collective-permute-start.23) | collective-permute-done | bytes 278560 | tf_op jit(solution)/shard_map/ppermute | solution.py:31
  118.3 3.3 %collective-permute-start.26 = (bf16[5,32,256]{2,1,0:T(8,128)(2,1)S(1)}, bf16[5,32,256]{2,1,0:T(8,128)(2,1)S(1)}, u32[]{:S(2)}, u32[]{:S(2)}) collective-permute-start(bf16[5,32,256]{2,1,0:T(8,128)(2,1)S(1)} %get-tuple-element.32), channel_id=1, source_target_pairs={{0,2},{1,3},{2,0},{3,1},{4,6},{5,7},{6,4},{7,5},{8,10},{9,11},{10,... | collective-permute-start | bytes 245768 | tf_op jit(solution)/shard_map/ppermute | solution.py:26
  121.6 2.3 %collective-permute-start.27 = (bf16[5,32,256]{2,1,0:T(8,128)(2,1)S(1)}, bf16[5,32,256]{2,1,0:T(8,128)(2,1)S(1)}, u32[]{:S(2)}, u32[]{:S(2)}) collective-permute-start(bf16[5,32,256]{2,1,0:T(8,128)(2,1)S(1)} %concatenate.75), channel_id=1, source_target_pairs={{0,3},{1,0},{2,1},{3,2},{4,7},{5,4},{6,5},{7,6},{8,11},{9,8},{10,9... | collective-permute-start | bytes 245768 | tf_op jit(solution)/shard_map/ppermute | solution.py:26
  124.0 1.9 %collective-permute-start = (s32[17]{0:T(128)S(1)}, s32[17]{0:T(128)S(1)}, u32[]{:S(2)}, u32[]{:S(2)}) collective-permute-start(s32[17]{0:T(128)S(1)} %pad_add_fusion.1), channel_id=1, source_target_pairs={{0,4},{4,8},{8,12},{12,16},{16,20},{20,24},{24,28},{1,5},{5,9},{9,... | collective-permute-start | bytes 212 | tf_op jit(solution)/shard_map/ppermute | solution.py:21
  125.9 2.7 %collective-permute-done.above = s32[17]{0:T(128)S(1)} collective-permute-done((s32[17]{0:T(128)S(1)}, s32[17]{0:T(128)S(1)}, u32[]{:S(2)}, u32[]{:S(2)}) %collective-permute-start) | collective-permute-done | bytes 100 | tf_op jit(solution)/shard_map/ppermute | solution.py:21
  129.2 2.9 %illumination.1 = f32[256,256]{1,0:T(8,128)} custom-call(s32[19]{0:T(128)} %pad_add_fusion.refs_0_.meta, s32[17]{0:T(128)} %copy-done.16, f32[256,256]{1,0:T(8,128)} %get-tuple-element.17.power), custom_call_target="tpu_custom_call" | custom-call | tf_op jit(solution)/shard_map/illumination/pallas_call | solution.py:338
  132.1 0.8 copy-done.7
  132.9 3.1 %rims.1 = (f32[2,256,256]{2,1,0:T(8,128)}, bf16[2,256,256]{2,1,0:T(8,128)(2,1)}, bf16[2,256,256]{2,1,0:T(8,128)(2,1)}, bf16[2,256,256]{2,1,0:T(8,128)(2,1)}) custom-call(s32[19]{0:T(128)} %pad_add_fusion.refs_0_.meta, s32[17]{0:T(128)} %copy-done.16, bf16[2,256,1024]{2,1,0:T(8,128)(2,1)} %get-tuple-element.11.main, bf16[2,2,256,256]{3,2,1,0:T(8,128)(2,1)} %copy-done.7), custom_call_target="tpu_custom_call" | custom-call | tf_op jit(solution)/shard_map/rims/pallas_call | solution.py:325
  136.4 2.1 %collective-permute-start.20 = (bf16[2,256,256]{2,1,0:T(8,128)(2,1)}, bf16[2,256,256]{2,1,0:T(8,128)(2,1)S(1)}, u32[]{:S(2)}, u32[]{:S(2)}) collective-permute-start(bf16[2,256,256]{2,1,0:T(8,128)(2,1)} %get-tuple-element.16), channel_id=1, source_target_pairs={{0,3},{1,0},{2,1},{3,2},{4,7},{5,4},{6,5},{7,6},{8,11},{9,8},{10,9... | collective-permute-start | bytes 786440 | tf_op jit(solution)/shard_map/ppermute | solution.py:26
  138.6 2.9 %collective-permute-start.30 = (f32[4,32,256]{2,1,0:T(8,128)S(1)}, f32[4,32,256]{2,1,0:T(8,128)S(1)}, u32[]{:S(2)}, u32[]{:S(2)}) collective-permute-start(f32[4,32,256]{2,1,0:T(8,128)S(1)} %slice_divide_fusion.refs_0_), channel_id=1, source_target_pairs={{0,24},{4,28},{8,16},{12,20},{16,8},{20,12},{24,0},{28,4},{1,25},{... | collective-permute-start | bytes 393224 | tf_op jit(solution)/shard_map/ppermute | solution.py:31
  141.5 4.9 %collective-permute-done.18 = bf16[2,256,256]{2,1,0:T(8,128)(2,1)S(1)} collective-permute-done((bf16[2,256,256]{2,1,0:T(8,128)(2,1)}, bf16[2,256,256]{2,1,0:T(8,128)(2,1)S(1)}, u32[]{:S(2)}, u32[]{:S(2)}) %collective-permute-start.18) | collective-permute-done | bytes 262176 | tf_op jit(solution)/shard_map/ppermute | solution.py:26
  146.4 7.0 %collective-permute-done.19 = bf16[2,256,256]{2,1,0:T(8,128)(2,1)S(1)} collective-permute-done((bf16[2,256,256]{2,1,0:T(8,128)(2,1)}, bf16[2,256,256]{2,1,0:T(8,128)(2,1)S(1)}, u32[]{:S(2)}, u32[]{:S(2)}) %collective-permute-start.19) | collective-permute-done | bytes 262176 | tf_op jit(solution)/shard_map/ppermute | solution.py:26
  153.4 4.6 %collective-permute-start.31 = (f32[4,32,256]{2,1,0:T(8,128)S(1)}, f32[4,32,256]{2,1,0:T(8,128)S(1)}, u32[]{:S(2)}, u32[]{:S(2)}) collective-permute-start(f32[4,32,256]{2,1,0:T(8,128)S(1)} %slice_divide_fusion.refs_0_), channel_id=1, source_target_pairs={{0,4},{4,0},{8,12},{12,8},{16,20},{20,16},{24,28},{28,24},{1,5},{5... | collective-permute-start | bytes 393224 | tf_op jit(solution)/shard_map/ppermute | solution.py:31
  158.6 4.3 %collective-permute-start.32 = (f32[4,32,256]{2,1,0:T(8,128)S(1)}, f32[4,32,256]{2,1,0:T(8,128)S(1)}, u32[]{:S(2)}, u32[]{:S(2)}) collective-permute-start(f32[4,32,256]{2,1,0:T(8,128)S(1)} %collective-permute-done.28.refs_1_), channel_id=1, source_target_pairs={{0,4},{4,0},{8,12},{12,8},{16,20},{20,16},{24,28},{28,24},{1,5},{5... | collective-permute-start | bytes 393224 | tf_op jit(solution)/shard_map/ppermute | solution.py:31
  162.9 2.0 %divide_add_fusion = f32[2,256,256]{2,1,0:T(8,128)} fusion(f32[2,256,256]{2,1,0:T(8,128)S(1)} %copy-done.2, bf16[2,256,256]{2,1,0:T(8,128)(2,1)S(1)} %collective-permute-done.20, bf16[2,256,256]{2,1,0:T(8,128)(2,1)S(1)} %collective-permute-done.19, f32[2,256,256]{2,1,0:T(8,128)} %get-tuple-element.13, bf16[2,256,256]{2,1,0:T(8,128)(2,1)S(1)} %collective-permute-done.18, ...), kind=kLoop, calls=%fused_computation.7 | loop fusion | flops 1048576 | bytes 2621440 | tf_op jit(solution)/shard_map/add | solution.py:346
  165.7 0.6 copy-done.15
  166.3 2.3 %join.1 = f32[2,2,256,256]{3,2,1,0:T(8,128)} custom-call(s32[19]{0:T(128)} %pad_add_fusion.refs_0_.meta, f32[4,32,256]{2,1,0:T(8,128)} %copy-done.6, f32[4,32,256]{2,1,0:T(8,128)} %copy-done.11, f32[4,32,256]{2,1,0:T(8,128)} %copy-done.10, f32[4,32,256]{2,1,0:T(8,128)} %copy-done.9, f32[4,32,256]{2,1,0:T(8,128)} %copy-done.12, f32[4,32,256]{2,1,0:T(8,128)} %copy-done.15, ...), custom_call_target="tpu_custom_call" | custom-call | tf_op jit(solution)/shard_map/join/pallas_call | solution.py:364
  (90 shorter events, 4.2 us)
Async XLA Ops:
  0.6 22.4 %copy-start.2 = (f32[2,256,256]{2,1,0:T(8,128)S(1)}, f32[2,256,256]{2,1,0:T(8,128)}, u32[]{:S(2)}) copy-start(f32[2,256,256]{2,1,0:T(8,128)} %param.7) | copy-start | bytes 1572868
  1.6 4.4 %collective-permute-start.10 = (f32[2,2,32,256]{3,2,1,0:T(8,128)S(1)}, f32[2,2,32,256]{3,2,1,0:T(8,128)S(1)}, u32[]{:S(2)}, u32[]{:S(2)}) collective-permute-start(f32[2,2,32,256]{3,2,1,0:T(8,128)S(1)} %constant_dynamic-slice_fusion), channel_id=1, source_target_pairs={{0,3},{1,0},{2,1},{3,2},{4,7},{5,4},{6,5},{7,6},{8,11},{9,8},{10,9... | collective-permute-start | bytes 393224 | tf_op jit(solution)/shard_map/ppermute | solution.py:26
  1.9 11.2 %collective-permute-start.9 = (f32[2,2,32,256]{3,2,1,0:T(8,128)S(1)}, f32[2,2,32,256]{3,2,1,0:T(8,128)S(1)}, u32[]{:S(2)}, u32[]{:S(2)}) collective-permute-start(f32[2,2,32,256]{3,2,1,0:T(8,128)S(1)} %constant_dynamic-slice_fusion), channel_id=1, source_target_pairs={{0,2},{1,3},{2,0},{3,1},{4,6},{5,7},{6,4},{7,5},{8,10},{9,11},{10,... | collective-permute-start | bytes 393224 | tf_op jit(solution)/shard_map/ppermute | solution.py:26
  5.1 10.9 %collective-permute-start.8 = (f32[2,2,32,256]{3,2,1,0:T(8,128)S(1)}, f32[2,2,32,256]{3,2,1,0:T(8,128)S(1)}, u32[]{:S(2)}, u32[]{:S(2)}) collective-permute-start(f32[2,2,32,256]{3,2,1,0:T(8,128)S(1)} %constant_dynamic-slice_fusion), channel_id=1, source_target_pairs={{0,1},{1,2},{2,3},{3,0},{4,5},{5,6},{6,7},{7,4},{8,9},{9,10},{10,1... | collective-permute-start | bytes 393224 | tf_op jit(solution)/shard_map/ppermute | solution.py:26
  16.1 5.3 %collective-permute-start.11 = (f32[1,3,1,2,32,256]{5,4,3,2,1,0:T(8,128)S(1)}, f32[1,3,1,2,32,256]{5,4,3,2,1,0:T(8,128)S(1)}, u32[]{:S(2)}, u32[]{:S(2)}) collective-permute-start(f32[1,3,1,2,32,256]{5,4,3,2,1,0:T(8,128)S(1)} %get-tuple-element.28), channel_id=1, source_target_pairs={{0,8},{4,12},{8,0},{12,4},{16,24},{20,28},{24,16},{28,20},{1,9},{5... | collective-permute-start | bytes 589832 | tf_op jit(solution)/shard_map/ppermute | solution.py:31
  17.3 5.0 %collective-permute-start.14 = (f32[1,3,1,2,32,256]{5,4,3,2,1,0:T(8,128)S(1)}, f32[1,3,1,2,32,256]{5,4,3,2,1,0:T(8,128)S(1)}, u32[]{:S(2)}, u32[]{:S(2)}) collective-permute-start(f32[1,3,1,2,32,256]{5,4,3,2,1,0:T(8,128)S(1)} %get-tuple-element.27), channel_id=1, source_target_pairs={{0,16},{4,20},{8,24},{12,28},{16,0},{20,4},{24,8},{28,12},{1,17},{... | collective-permute-start | bytes 589832 | tf_op jit(solution)/shard_map/ppermute | solution.py:31
  21.4 41.8 %copy-start.17 = (s32[8,2]{0,1:T(2,128)S(1)}, s32[8,2]{0,1:T(2,128)}, u32[]{:S(2)}) copy-start(s32[8,2]{0,1:T(2,128)} %param.10) | copy-start | bytes 196
  21.4 8.8 %collective-permute-start.12 = (f32[2,3,1,2,32,256]{5,4,3,2,1,0:T(8,128)S(1)}, f32[2,3,1,2,32,256]{5,4,3,2,1,0:T(8,128)S(1)}, u32[]{:S(2)}, u32[]{:S(2)}) collective-permute-start(f32[2,3,1,2,32,256]{5,4,3,2,1,0:T(8,128)S(1)} %pad_maximum_fusion.2), channel_id=1, source_target_pairs={{0,16},{4,20},{8,24},{12,28},{16,0},{20,4},{24,8},{28,12},{1,17},{... | collective-permute-start | bytes 1179656 | tf_op jit(solution)/shard_map/ppermute | solution.py:31
  22.3 10.9 %collective-permute-start.15 = (f32[2,3,1,2,32,256]{5,4,3,2,1,0:T(8,128)S(1)}, f32[2,3,1,2,32,256]{5,4,3,2,1,0:T(8,128)S(1)}, u32[]{:S(2)}, u32[]{:S(2)}) collective-permute-start(f32[2,3,1,2,32,256]{5,4,3,2,1,0:T(8,128)S(1)} %pad_maximum_fusion.3), channel_id=1, source_target_pairs={{0,8},{4,12},{8,0},{12,4},{16,24},{20,28},{24,16},{28,20},{1,9},{5... | collective-permute-start | bytes 1179656 | tf_op jit(solution)/shard_map/ppermute | solution.py:31
  23.0 44.6 %copy-start.3 = (bf16[2,256,256]{2,1,0:T(8,128)(2,1)}, bf16[2,256,256]{2,1,0:T(8,128)(2,1)S(1)}, u32[]{:S(2)}) copy-start(bf16[2,256,256]{2,1,0:T(8,128)(2,1)S(1)} %convert_element_type.48.refs_1_) | copy-start | bytes 786436
  23.0 13.0 %collective-permute-start.4 = (bf16[2,256,256]{2,1,0:T(8,128)(2,1)S(1)}, bf16[2,256,256]{2,1,0:T(8,128)(2,1)S(1)}, u32[]{:S(2)}, u32[]{:S(2)}) collective-permute-start(bf16[2,256,256]{2,1,0:T(8,128)(2,1)S(1)} %convert_element_type.48.refs_1_), channel_id=1, source_target_pairs={{4,0},{8,4},{12,8},{16,12},{20,16},{24,20},{28,24},{5,1},{9,5},{13... | collective-permute-start | bytes 786440 | tf_op jit(solution)/shard_map/ppermute | solution.py:21
  30.3 37.3 %copy-start = (f32[4,3,1,2,32,256]{5,4,3,2,1,0:T(8,128)}, f32[4,3,1,2,32,256]{5,4,3,2,1,0:T(8,128)S(1)}, u32[]{:S(2)}) copy-start(f32[4,3,1,2,32,256]{5,4,3,2,1,0:T(8,128)S(1)} %pad_maximum_fusion.refs_10_) | copy-start | bytes 2359300
  30.3 37.3 %collective-permute-start.13 = (f32[4,3,1,2,32,256]{5,4,3,2,1,0:T(8,128)S(1)}, f32[4,3,1,2,32,256]{5,4,3,2,1,0:T(8,128)S(1)}, u32[]{:S(2)}, u32[]{:S(2)}) collective-permute-start(f32[4,3,1,2,32,256]{5,4,3,2,1,0:T(8,128)S(1)} %pad_maximum_fusion.refs_10_), channel_id=1, source_target_pairs={{0,4},{4,0},{8,12},{12,8},{16,20},{20,16},{24,28},{28,24},{1,5},{5... | collective-permute-start | bytes 2359304 | tf_op jit(solution)/shard_map/ppermute | solution.py:31
  33.3 34.3 %copy-start.1 = (f32[4,3,1,2,32,256]{5,4,3,2,1,0:T(8,128)}, f32[4,3,1,2,32,256]{5,4,3,2,1,0:T(8,128)S(1)}, u32[]{:S(2)}) copy-start(f32[4,3,1,2,32,256]{5,4,3,2,1,0:T(8,128)S(1)} %pad_maximum_fusion.1.refs_12_) | copy-start | bytes 2359300
  33.3 34.3 %collective-permute-start.16 = (f32[4,3,1,2,32,256]{5,4,3,2,1,0:T(8,128)S(1)}, f32[4,3,1,2,32,256]{5,4,3,2,1,0:T(8,128)}, u32[]{:S(2)}, u32[]{:S(2)}) collective-permute-start(f32[4,3,1,2,32,256]{5,4,3,2,1,0:T(8,128)S(1)} %pad_maximum_fusion.1.refs_12_), channel_id=1, source_target_pairs={{0,4},{4,0},{8,12},{12,8},{16,20},{20,16},{24,28},{28,24},{1,5},{5... | collective-permute-start | bytes 2359304 | tf_op jit(solution)/shard_map/ppermute | solution.py:31
  34.0 7.9 %collective-permute-start.3 = (bf16[2,256,256]{2,1,0:T(8,128)(2,1)S(1)}, bf16[2,256,256]{2,1,0:T(8,128)(2,1)}, u32[]{:S(2)}, u32[]{:S(2)}) collective-permute-start(bf16[2,256,256]{2,1,0:T(8,128)(2,1)S(1)} %convert_element_type.48.refs_1_), channel_id=1, source_target_pairs={{0,3},{1,0},{2,1},{3,2},{4,7},{5,4},{6,5},{7,6},{8,11},{9,8},{10,9... | collective-permute-start | bytes 786440 | tf_op jit(solution)/shard_map/ppermute | solution.py:26
  34.1 22.7 %collective-permute-start.2 = (bf16[2,256,256]{2,1,0:T(8,128)(2,1)S(1)}, bf16[2,256,256]{2,1,0:T(8,128)(2,1)}, u32[]{:S(2)}, u32[]{:S(2)}) collective-permute-start(bf16[2,256,256]{2,1,0:T(8,128)(2,1)S(1)} %convert_element_type.48.refs_1_), channel_id=1, source_target_pairs={{0,2},{1,3},{2,0},{3,1},{4,6},{5,7},{6,4},{7,5},{8,10},{9,11},{10,... | collective-permute-start | bytes 786440 | tf_op jit(solution)/shard_map/ppermute | solution.py:26
  36.0 31.6 %copy-start.8 = (bf16[2,256,256]{2,1,0:T(8,128)(2,1)}, bf16[2,256,256]{2,1,0:T(8,128)(2,1)S(1)}, u32[]{:S(2)}) copy-start(bf16[2,256,256]{2,1,0:T(8,128)(2,1)S(1)} %collective-permute-done.4.refs_5_) | copy-start | bytes 786436
  36.0 23.3 %collective-permute-start.1 = (bf16[2,256,256]{2,1,0:T(8,128)(2,1)S(1)}, bf16[2,256,256]{2,1,0:T(8,128)(2,1)}, u32[]{:S(2)}, u32[]{:S(2)}) collective-permute-start(bf16[2,256,256]{2,1,0:T(8,128)(2,1)S(1)} %convert_element_type.48.refs_1_), channel_id=1, source_target_pairs={{0,1},{1,2},{2,3},{3,0},{4,5},{5,6},{6,7},{7,4},{8,9},{9,10},{10,1... | collective-permute-start | bytes 786440 | tf_op jit(solution)/shard_map/ppermute | solution.py:26
  41.9 22.1 %collective-permute-start.7 = (bf16[2,256,256]{2,1,0:T(8,128)(2,1)}, bf16[2,256,256]{2,1,0:T(8,128)(2,1)}, u32[]{:S(2)}, u32[]{:S(2)}) collective-permute-start(bf16[2,256,256]{2,1,0:T(8,128)(2,1)} %collective-permute-done.3.refs_4_), channel_id=1, source_target_pairs={{4,0},{8,4},{12,8},{16,12},{20,16},{24,20},{28,24},{5,1},{9,5},{13... | collective-permute-start | bytes 786440 | tf_op jit(solution)/shard_map/ppermute | solution.py:21
  56.8 8.0 %collective-permute-start.6 = (bf16[2,256,256]{2,1,0:T(8,128)(2,1)}, bf16[2,256,256]{2,1,0:T(8,128)(2,1)}, u32[]{:S(2)}, u32[]{:S(2)}) collective-permute-start(bf16[2,256,256]{2,1,0:T(8,128)(2,1)} %collective-permute-done.2.refs_3_), channel_id=1, source_target_pairs={{4,0},{8,4},{12,8},{16,12},{20,16},{24,20},{28,24},{5,1},{9,5},{13... | collective-permute-start | bytes 786440 | tf_op jit(solution)/shard_map/ppermute | solution.py:21
  59.3 8.2 %collective-permute-start.5 = (bf16[2,256,256]{2,1,0:T(8,128)(2,1)}, bf16[2,256,256]{2,1,0:T(8,128)(2,1)}, u32[]{:S(2)}, u32[]{:S(2)}) collective-permute-start(bf16[2,256,256]{2,1,0:T(8,128)(2,1)} %collective-permute-done.1.refs_2_), channel_id=1, source_target_pairs={{4,0},{8,4},{12,8},{16,12},{20,16},{24,20},{28,24},{5,1},{9,5},{13... | collective-permute-start | bytes 786440 | tf_op jit(solution)/shard_map/ppermute | solution.py:21
  67.6 0.9 copy-start.5
  90.8 3.0 %collective-permute-start.21 = (bf16[4,17,32,256]{3,2,1,0:T(8,128)(2,1)}, bf16[4,17,32,256]{3,2,1,0:T(8,128)(2,1)S(1)}, u32[]{:S(2)}, u32[]{:S(2)}) collective-permute-start(bf16[4,17,32,256]{3,2,1,0:T(8,128)(2,1)} %get-tuple-element.19), channel_id=1, source_target_pairs={{0,4},{4,0},{8,12},{12,8},{16,20},{20,16},{24,28},{28,24},{1,5},{5... | collective-permute-start | bytes 3342344 | tf_op jit(solution)/shard_map/ppermute | solution.py:31
  93.8 5.1 %copy-start.18 = (bf16[2,2,256,256]{3,2,1,0:T(8,128)(2,1)S(1)}, bf16[2,2,256,256]{3,2,1,0:T(8,128)(2,1)}, u32[]{:S(2)}) copy-start(bf16[2,2,256,256]{3,2,1,0:T(8,128)(2,1)} %get-tuple-element.12) | copy-start | bytes 1572868
  96.0 8.1 %collective-permute-start.22 = (bf16[17,32,256]{2,1,0:T(8,128)(2,1)S(1)}, bf16[17,32,256]{2,1,0:T(8,128)(2,1)S(1)}, u32[]{:S(2)}, u32[]{:S(2)}) collective-permute-start(bf16[17,32,256]{2,1,0:T(8,128)(2,1)S(1)} %get-tuple-element.24), channel_id=1, source_target_pairs={{0,8},{4,12},{8,0},{12,4},{16,24},{20,28},{24,16},{28,20},{1,9},{5... | collective-permute-start | bytes 835592 | tf_op jit(solution)/shard_map/ppermute | solution.py:31
  96.1 15.4 %collective-permute-start.24 = (bf16[17,32,256]{2,1,0:T(8,128)(2,1)S(1)}, bf16[17,32,256]{2,1,0:T(8,128)(2,1)S(1)}, u32[]{:S(2)}, u32[]{:S(2)}) collective-permute-start(bf16[17,32,256]{2,1,0:T(8,128)(2,1)S(1)} %get-tuple-element.25), channel_id=1, source_target_pairs={{0,24},{4,28},{8,16},{12,20},{16,8},{20,12},{24,0},{28,4},{1,25},{... | collective-permute-start | bytes 835592 | tf_op jit(solution)/shard_map/ppermute | solution.py:31
  98.6 19.4 %collective-permute-start.23 = (bf16[17,32,256]{2,1,0:T(8,128)(2,1)S(1)}, bf16[17,32,256]{2,1,0:T(8,128)(2,1)S(1)}, u32[]{:S(2)}, u32[]{:S(2)}) collective-permute-start(bf16[17,32,256]{2,1,0:T(8,128)(2,1)S(1)} %get-tuple-element.26), channel_id=1, source_target_pairs={{0,16},{4,20},{8,24},{12,28},{16,0},{20,4},{24,8},{28,12},{1,17},{... | collective-permute-start | bytes 835592 | tf_op jit(solution)/shard_map/ppermute | solution.py:31
  98.8 33.2 %collective-permute-start.17 = (bf16[2,2,256,256]{3,2,1,0:T(8,128)(2,1)S(1)}, bf16[2,2,256,256]{3,2,1,0:T(8,128)(2,1)S(1)}, u32[]{:S(2)}, u32[]{:S(2)}) collective-permute-start(bf16[2,2,256,256]{3,2,1,0:T(8,128)(2,1)S(1)} %copy-done.18), channel_id=1, source_target_pairs={{0,4},{4,8},{8,12},{12,16},{16,20},{20,24},{24,28},{1,5},{5,9},{9,... | collective-permute-start | bytes 1572872 | tf_op jit(solution)/shard_map/ppermute | solution.py:21
  118.3 18.1 %collective-permute-start.25 = (bf16[5,32,256]{2,1,0:T(8,128)(2,1)S(1)}, bf16[5,32,256]{2,1,0:T(8,128)(2,1)S(1)}, u32[]{:S(2)}, u32[]{:S(2)}) collective-permute-start(bf16[5,32,256]{2,1,0:T(8,128)(2,1)S(1)} %get-tuple-element.31), channel_id=1, source_target_pairs={{0,1},{1,2},{2,3},{3,0},{4,5},{5,6},{6,7},{7,4},{8,9},{9,10},{10,1... | collective-permute-start | bytes 245768 | tf_op jit(solution)/shard_map/ppermute | solution.py:26
  118.3 20.1 %collective-permute-start.26 = (bf16[5,32,256]{2,1,0:T(8,128)(2,1)S(1)}, bf16[5,32,256]{2,1,0:T(8,128)(2,1)S(1)}, u32[]{:S(2)}, u32[]{:S(2)}) collective-permute-start(bf16[5,32,256]{2,1,0:T(8,128)(2,1)S(1)} %get-tuple-element.32), channel_id=1, source_target_pairs={{0,2},{1,3},{2,0},{3,1},{4,6},{5,7},{6,4},{7,5},{8,10},{9,11},{10,... | collective-permute-start | bytes 245768 | tf_op jit(solution)/shard_map/ppermute | solution.py:26
  121.6 16.8 %collective-permute-start.27 = (bf16[5,32,256]{2,1,0:T(8,128)(2,1)S(1)}, bf16[5,32,256]{2,1,0:T(8,128)(2,1)S(1)}, u32[]{:S(2)}, u32[]{:S(2)}) collective-permute-start(bf16[5,32,256]{2,1,0:T(8,128)(2,1)S(1)} %concatenate.75), channel_id=1, source_target_pairs={{0,3},{1,0},{2,1},{3,2},{4,7},{5,4},{6,5},{7,6},{8,11},{9,8},{10,9... | collective-permute-start | bytes 245768 | tf_op jit(solution)/shard_map/ppermute | solution.py:26
  124.0 4.7 %collective-permute-start = (s32[17]{0:T(128)S(1)}, s32[17]{0:T(128)S(1)}, u32[]{:S(2)}, u32[]{:S(2)}) collective-permute-start(s32[17]{0:T(128)S(1)} %pad_add_fusion.1), channel_id=1, source_target_pairs={{0,4},{4,8},{8,12},{12,16},{16,20},{20,24},{24,28},{1,5},{5,9},{9,... | collective-permute-start | bytes 212 | tf_op jit(solution)/shard_map/ppermute | solution.py:21
  132.1 14.4 %copy-start.4 = (f32[256,256]{1,0:T(8,128)S(1)}, f32[256,256]{1,0:T(8,128)}, u32[]{:S(2)}) copy-start(f32[256,256]{1,0:T(8,128)} %illumination.1) | copy-start | bytes 786436
  135.9 10.5 %collective-permute-start.18 = (bf16[2,256,256]{2,1,0:T(8,128)(2,1)}, bf16[2,256,256]{2,1,0:T(8,128)(2,1)S(1)}, u32[]{:S(2)}, u32[]{:S(2)}) collective-permute-start(bf16[2,256,256]{2,1,0:T(8,128)(2,1)} %get-tuple-element.14), channel_id=1, source_target_pairs={{0,1},{1,2},{2,3},{3,0},{4,5},{5,6},{6,7},{7,4},{8,9},{9,10},{10,1... | collective-permute-start | bytes 786440 | tf_op jit(solution)/shard_map/ppermute | solution.py:26
  135.9 17.5 %collective-permute-start.19 = (bf16[2,256,256]{2,1,0:T(8,128)(2,1)}, bf16[2,256,256]{2,1,0:T(8,128)(2,1)S(1)}, u32[]{:S(2)}, u32[]{:S(2)}) collective-permute-start(bf16[2,256,256]{2,1,0:T(8,128)(2,1)} %get-tuple-element.15), channel_id=1, source_target_pairs={{0,2},{1,3},{2,0},{3,1},{4,6},{5,7},{6,4},{7,5},{8,10},{9,11},{10,... | collective-permute-start | bytes 786440 | tf_op jit(solution)/shard_map/ppermute | solution.py:26
  136.4 26.6 %collective-permute-start.20 = (bf16[2,256,256]{2,1,0:T(8,128)(2,1)}, bf16[2,256,256]{2,1,0:T(8,128)(2,1)S(1)}, u32[]{:S(2)}, u32[]{:S(2)}) collective-permute-start(bf16[2,256,256]{2,1,0:T(8,128)(2,1)} %get-tuple-element.16), channel_id=1, source_target_pairs={{0,3},{1,0},{2,1},{3,2},{4,7},{5,4},{6,5},{7,6},{8,11},{9,8},{10,9... | collective-permute-start | bytes 786440 | tf_op jit(solution)/shard_map/ppermute | solution.py:26
  138.5 26.4 %copy-start.6 = (f32[4,32,256]{2,1,0:T(8,128)}, f32[4,32,256]{2,1,0:T(8,128)S(1)}, u32[]{:S(2)}) copy-start(f32[4,32,256]{2,1,0:T(8,128)S(1)} %slice_divide_fusion.refs_0_) | copy-start | bytes 393220
  138.6 19.5 %collective-permute-start.30 = (f32[4,32,256]{2,1,0:T(8,128)S(1)}, f32[4,32,256]{2,1,0:T(8,128)S(1)}, u32[]{:S(2)}, u32[]{:S(2)}) collective-permute-start(f32[4,32,256]{2,1,0:T(8,128)S(1)} %slice_divide_fusion.refs_0_), channel_id=1, source_target_pairs={{0,24},{4,28},{8,16},{12,20},{16,8},{20,12},{24,0},{28,4},{1,25},{... | collective-permute-start | bytes 393224 | tf_op jit(solution)/shard_map/ppermute | solution.py:31
  141.5 16.7 %collective-permute-start.29 = (f32[4,32,256]{2,1,0:T(8,128)S(1)}, f32[4,32,256]{2,1,0:T(8,128)S(1)}, u32[]{:S(2)}, u32[]{:S(2)}) collective-permute-start(f32[4,32,256]{2,1,0:T(8,128)S(1)} %slice_divide_fusion.refs_0_), channel_id=1, source_target_pairs={{0,16},{4,20},{8,24},{12,28},{16,0},{20,4},{24,8},{28,12},{1,17},{... | collective-permute-start | bytes 393224 | tf_op jit(solution)/shard_map/ppermute | solution.py:31
  146.4 12.2 %collective-permute-start.28 = (f32[4,32,256]{2,1,0:T(8,128)S(1)}, f32[4,32,256]{2,1,0:T(8,128)S(1)}, u32[]{:S(2)}, u32[]{:S(2)}) collective-permute-start(f32[4,32,256]{2,1,0:T(8,128)S(1)} %slice_divide_fusion.refs_0_), channel_id=1, source_target_pairs={{0,8},{4,12},{8,0},{12,4},{16,24},{20,28},{24,16},{28,20},{1,9},{5... | collective-permute-start | bytes 393224 | tf_op jit(solution)/shard_map/ppermute | solution.py:31
  153.4 11.5 %collective-permute-start.31 = (f32[4,32,256]{2,1,0:T(8,128)S(1)}, f32[4,32,256]{2,1,0:T(8,128)S(1)}, u32[]{:S(2)}, u32[]{:S(2)}) collective-permute-start(f32[4,32,256]{2,1,0:T(8,128)S(1)} %slice_divide_fusion.refs_0_), channel_id=1, source_target_pairs={{0,4},{4,0},{8,12},{12,8},{16,20},{20,16},{24,28},{28,24},{1,5},{5... | collective-permute-start | bytes 393224 | tf_op jit(solution)/shard_map/ppermute | solution.py:31
  158.0 6.9 %copy-start.9 = (f32[4,32,256]{2,1,0:T(8,128)}, f32[4,32,256]{2,1,0:T(8,128)S(1)}, u32[]{:S(2)}) copy-start(f32[4,32,256]{2,1,0:T(8,128)S(1)} %collective-permute-done.30.refs_3_) | copy-start | bytes 393220
  158.0 6.9 %collective-permute-start.34 = (f32[4,32,256]{2,1,0:T(8,128)S(1)}, f32[4,32,256]{2,1,0:T(8,128)S(1)}, u32[]{:S(2)}, u32[]{:S(2)}) collective-permute-start(f32[4,32,256]{2,1,0:T(8,128)S(1)} %collective-permute-done.30.refs_3_), channel_id=1, source_target_pairs={{0,4},{4,0},{8,12},{12,8},{16,20},{20,16},{24,28},{28,24},{1,5},{5... | collective-permute-start | bytes 393224 | tf_op jit(solution)/shard_map/ppermute | solution.py:31
  158.1 6.8 %copy-start.10 = (f32[4,32,256]{2,1,0:T(8,128)}, f32[4,32,256]{2,1,0:T(8,128)S(1)}, u32[]{:S(2)}) copy-start(f32[4,32,256]{2,1,0:T(8,128)S(1)} %collective-permute-done.29.refs_2_) | copy-start | bytes 393220
  158.1 6.8 %collective-permute-start.33 = (f32[4,32,256]{2,1,0:T(8,128)S(1)}, f32[4,32,256]{2,1,0:T(8,128)S(1)}, u32[]{:S(2)}, u32[]{:S(2)}) collective-permute-start(f32[4,32,256]{2,1,0:T(8,128)S(1)} %collective-permute-done.29.refs_2_), channel_id=1, source_target_pairs={{0,4},{4,0},{8,12},{12,8},{16,20},{20,16},{24,28},{28,24},{1,5},{5... | collective-permute-start | bytes 393224 | tf_op jit(solution)/shard_map/ppermute | solution.py:31
  158.6 6.4 %copy-start.11 = (f32[4,32,256]{2,1,0:T(8,128)}, f32[4,32,256]{2,1,0:T(8,128)S(1)}, u32[]{:S(2)}) copy-start(f32[4,32,256]{2,1,0:T(8,128)S(1)} %collective-permute-done.28.refs_1_) | copy-start | bytes 393220
  158.6 6.4 %collective-permute-start.32 = (f32[4,32,256]{2,1,0:T(8,128)S(1)}, f32[4,32,256]{2,1,0:T(8,128)S(1)}, u32[]{:S(2)}, u32[]{:S(2)}) collective-permute-start(f32[4,32,256]{2,1,0:T(8,128)S(1)} %collective-permute-done.28.refs_1_), channel_id=1, source_target_pairs={{0,4},{4,0},{8,12},{12,8},{16,20},{20,16},{24,28},{28,24},{1,5},{5... | collective-permute-start | bytes 393224 | tf_op jit(solution)/shard_map/ppermute | solution.py:31
  (6 other events, 4.1 us)
